TPU v7x, 32 devices: a whole 2x2x4 slice. The times are simulated.
32 devices in a mesh: dp: 4 (over x, core), expert: 8 (over z, y).
Axes of the slice: x: 2, y: 2, z: 4, core: 2. Of those that a mesh axis runs over, the one named last changes fastest.
Arguments:
- tokens: bfloat16 [4096, 2048], P(('dp', 'expert')), may hold values from -6 to 6
- upstream: bfloat16 [4096, 2048], P(('dp', 'expert')), may hold values from -1.1953125 to 1.1953125
- expert_ids: int32 [4096, 3], P(('dp', 'expert')), may hold values from 0 to 7, all different within a row; in each aligned block of 128 rows (0 to 127, 128 to 255, ...) at most 64 rows name the same one
- gate_probs: float32 [4096, 3], P(('dp', 'expert')), may hold values from 0.05 to 1
- w_gate: bfloat16 [8, 2048, 704], P('expert'), may hold values from -0.125 to 0.125
- w_up: bfloat16 [8, 2048, 704], P('expert'), may hold values from -0.125 to 0.125
- w_down: bfloat16 [8, 704, 2048], P('expert'), may hold values from -0.21875 to 0.21875
Outputs:
- mixed: bfloat16 [4096, 2048], P(('dp', 'expert'))
- grad_probs: float32 [4096, 3], P(('dp', 'expert'))
- token_grad: bfloat16 [4096, 2048], P(('dp', 'expert'))
- grad_gate: float32 [8, 2048, 704], P('expert', 'dp')
- grad_up: float32 [8, 2048, 704], P('expert', 'dp')
- grad_down: float32 [8, 704, 2048], P('expert', None, 'dp')
Inputs may be any that keep to these rules, and one draw needn't show every extreme that they name: `expert_ids`: each token names 3 different experts. Within each aligned block of 128 tokens (the tokens of one device) at most 64 routes name one expert, and in some blocks one expert is named by exactly 64 routes.
All inputs are finite; a program needn't handle non-finite values.
Results may differ from a plain program's by a relative error of at most 0.015.
Values may be sent and summed in bfloat16 or wider, within the bound.
A program may use at most 128 MiB of HBM per device.

v0:
```python
import jax
import jax.numpy as jnp
from jax import lax
from jax.sharding import PartitionSpec as P


def contract_last(left, right):
    return lax.dot_general(
        left, right, (((1,), (1,)), ((), ())), preferred_element_type=jnp.float32
    )


def contract_rows(left, right):
    return lax.dot_general(
        left, right, (((0,), (0,)), ((), ())), preferred_element_type=jnp.float32
    )


def expert_forward(row_data, gate_matrix, up_matrix, down_matrix):
    gate_pre = jnp.dot(row_data, gate_matrix, preferred_element_type=jnp.float32)
    up_pre = jnp.dot(row_data, up_matrix, preferred_element_type=jnp.float32)
    hidden = (jax.nn.silu(gate_pre) * up_pre).astype(jnp.bfloat16)
    result = jnp.dot(hidden, down_matrix, preferred_element_type=jnp.float32).astype(jnp.bfloat16)
    return (result, gate_pre, up_pre, hidden)


def expert_backward(
    row_data, out_grad, gate_pre, up_pre, hidden, gate_matrix, up_matrix, down_matrix
):
    hidden_grad = contract_last(out_grad, down_matrix)
    sigmoid_gate = jax.nn.sigmoid(gate_pre)
    gate_grad = (
        hidden_grad * up_pre * sigmoid_gate * (1.0 + gate_pre * (1.0 - sigmoid_gate))
    ).astype(jnp.bfloat16)
    up_grad = (hidden_grad * gate_pre * sigmoid_gate).astype(jnp.bfloat16)
    route_grad = (contract_last(gate_grad, gate_matrix) + contract_last(up_grad, up_matrix)).astype(
        jnp.bfloat16
    )
    return (
        route_grad,
        contract_rows(row_data, gate_grad),
        contract_rows(row_data, up_grad),
        contract_rows(hidden, out_grad),
    )


def forward_padded(row_data, weights):
    result, gate_pre, up_pre, hidden = expert_forward(row_data, weights[0], weights[1], weights[2])
    return (result, (row_data, gate_pre, up_pre, hidden))


def backward_padded(saved_state, out_grad, weights):
    row_data, gate_pre, up_pre, hidden = saved_state
    return expert_backward(
        row_data, out_grad, gate_pre, up_pre, hidden, weights[0], weights[1], weights[2]
    )


def shards(tokens, upstream, expert_ids, gate_probs, w_gate, w_up, w_down):
    tok_rows, model_width = tokens.shape
    routes = expert_ids.shape[1]
    experts = lax.axis_size("expert")
    capacity = 4 * tok_rows * routes // (3 * experts)
    slots_total = experts * capacity
    flat_ids = expert_ids.reshape(-1)
    matches = (flat_ids[:, None] == jnp.arange(experts, dtype=jnp.int32)[None, :]).astype(jnp.int32)
    before = jnp.cumsum(matches, axis=0) - matches
    target = flat_ids * capacity + jnp.sum(before * matches, axis=1)

    def dispatch(values):
        buffer = jnp.zeros((slots_total, model_width), values.dtype).at[target].set(values)
        return buffer.reshape(experts, capacity, model_width)

    def collect(buffer):
        return buffer.reshape(slots_total, model_width)[target].reshape(
            tok_rows, routes, model_width
        )

    def flatten(buffer):
        return buffer.reshape(slots_total, model_width)

    def unflatten(array):
        return array.reshape(experts, capacity, model_width)

    token_copies = jnp.repeat(tokens, routes, axis=0)
    out_grad = (
        gate_probs.reshape(-1)[:, None] * jnp.repeat(upstream, routes, axis=0).astype(jnp.float32)
    ).astype(jnp.bfloat16)
    weights = (w_gate[0], w_up[0], w_down[0])
    sent_rows = lax.all_to_all(
        dispatch(token_copies), "expert", split_axis=0, concat_axis=0, tiled=True
    )
    result, saved_state = forward_padded(flatten(sent_rows), weights)
    back_out = lax.all_to_all(unflatten(result), "expert", split_axis=0, concat_axis=0, tiled=True)
    sent_grads = lax.all_to_all(
        dispatch(out_grad), "expert", split_axis=0, concat_axis=0, tiled=True
    )
    route_grad, gate_sum, up_sum, down_sum = backward_padded(
        saved_state, flatten(sent_grads), weights
    )
    back_grad = lax.all_to_all(
        unflatten(route_grad), "expert", split_axis=0, concat_axis=0, tiled=True
    )
    expert_out = collect(back_out).astype(jnp.float32)
    mixed = jnp.sum(gate_probs[:, :, None] * expert_out, axis=1).astype(jnp.bfloat16)
    grad_probs = jnp.sum(upstream[:, None, :].astype(jnp.float32) * expert_out, axis=2)
    token_grad = jnp.sum(collect(back_grad).astype(jnp.float32), axis=1).astype(jnp.bfloat16)
    grad_gate, grad_up, grad_down = (
        lax.psum_scatter(
            gate_sum[None].astype(jnp.bfloat16), "dp", scatter_dimension=1, tiled=True
        ).astype(jnp.float32),
        lax.psum_scatter(
            up_sum[None].astype(jnp.bfloat16), "dp", scatter_dimension=1, tiled=True
        ).astype(jnp.float32),
        lax.psum_scatter(
            down_sum[None].astype(jnp.bfloat16), "dp", scatter_dimension=2, tiled=True
        ).astype(jnp.float32),
    )
    return (mixed, grad_probs, token_grad, grad_gate, grad_up, grad_down)


def solution(mesh):
    placed = (
        P(("dp", "expert"), None),
        P(("dp", "expert"), None),
        P(("dp", "expert"), None),
        P(("dp", "expert"), None),
        P("expert", None, None),
        P("expert", None, None),
        P("expert", None, None),
    )
    return jax.shard_map(
        shards,
        mesh=mesh,
        in_specs=placed,
        out_specs=(
            P(("dp", "expert"), None),
            P(("dp", "expert"), None),
            P(("dp", "expert"), None),
            P("expert", "dp", None),
            P("expert", "dp", None),
            P("expert", None, "dp"),
        ),
        check_vma=False,
    )
```

profile of v0, /device:TPU:0, one launch (start us, length us, event | category | flops | bytes accessed | tf_op | source)
XLA Modules:
  0.0 294.9 jit_solution(12151211653655984824)
XLA Ops:
  7.2 0.9 copy.21
  8.1 0.2 eq.29
  8.3 0.2 eq.25
  8.5 0.7 broadcast_multiply_fusion
  9.2 0.8 reduce-window.6
  10.1 0.2 slice_reduce_fusion
  10.3 0.1 copy.20
  10.4 0.2 mul.77
  10.7 3.4 %broadcast_in_dim.2 = bf16[128,3,2048]{2,1,0:T(4,128)(2,1)} broadcast(bf16[128,2048]{1,0:T(8,128)(2,1)} %param.7), dimensions={0,2} | broadcast | bytes 2097152 | tf_op jit(solution)/shard_map/broadcast_in_dim | solution.py:85
  14.1 5.1 %reshape.142 = bf16[384,2048]{1,0:T(8,128)(2,1)} reshape(bf16[128,3,2048]{2,1,0:T(4,128)(2,1)} %broadcast_in_dim.2) | data formatting | bytes 3145728 | tf_op jit(solution)/shard_map/reshape | solution.py:85
  19.2 0.1 fusion.19
  19.3 5.3 %scatter_custom_fusion = bf16[512,2048]{1,0:T(8,128)(2,1)} fusion(s32[384]{0:T(512)S(1)} %fusion.21, bf16[384,2048]{1,0:T(8,128)(2,1)} %reshape.142, bf16[]{:T(256)} %constant.6.clone.1), kind=kCustom, calls=%fused_computation.32 | custom fusion | bytes 2097664 | tf_op jit(solution)/shard_map/scatter | solution.py:71
  24.6 7.4 %all-to-all-start = ((bf16[8,64,2048]{2,1,0:T(8,128)(2,1)}), bf16[8,64,2048]{2,1,0:T(8,128)(2,1)}, u32[]{:S(2)}, u32[]{:S(2)}) async-start(bf16[8,64,2048]{2,1,0:T(8,128)(2,1)} %bitcast.53), calls=%async_computation | async-start | bytes 4194304 | tf_op jit(solution)/shard_map/all_to_all | solution.py:90
  32.0 0.1 copy.19
  32.2 0.2 mul.84
  32.4 3.0 %mul.82 = f32[128,3,2048]{2,1,0:T(4,128)} broadcast(bf16[128,2048]{1,0:T(8,128)(2,1)S(1)} %copy-done.1), dimensions={0,2} | broadcast | bytes 3670016 | tf_op jit(solution)/shard_map/mul | solution.py:106
  35.3 6.0 %convert_element_type.84 = f32[384,2048]{1,0:T(8,128)} reshape(f32[128,3,2048]{2,1,0:T(4,128)} %mul.82) | data formatting | bytes 6291456 | tf_op jit(solution)/shard_map/convert_element_type | solution.py:87
  41.3 5.8 %scatter_custom_fusion.1 = bf16[512,2048]{1,0:T(8,128)(2,1)} fusion(s32[384]{0:T(512)S(1)} %fusion.21, f32[384,2048]{1,0:T(8,128)} %convert_element_type.84, f32[384]{0:T(512)S(1)} %mul.84, bf16[]{:T(256)} %constant.6.clone.1), kind=kCustom, calls=%fused_computation.25 | custom fusion | flops 1572864 | bytes 5244930 | tf_op jit(solution)/shard_map/scatter | solution.py:71
  47.1 33.3 %all-to-all-done = bf16[8,64,2048]{2,1,0:T(8,128)(2,1)} async-done(((bf16[8,64,2048]{2,1,0:T(8,128)(2,1)}), bf16[8,64,2048]{2,1,0:T(8,128)(2,1)}, u32[]{:S(2)}, u32[]{:S(2)}) %all-to-all-start) | async-done | bytes 2097184 | tf_op jit(solution)/shard_map/all_to_all | solution.py:90
  80.4 4.3 %all-to-all-start.2 = ((bf16[8,64,2048]{2,1,0:T(8,128)(2,1)}), bf16[8,64,2048]{2,1,0:T(8,128)(2,1)}, u32[]{:S(2)}, u32[]{:S(2)}) async-start(bf16[8,64,2048]{2,1,0:T(8,128)(2,1)} %bitcast.52), calls=%async_computation.2 | async-start | bytes 4194304 | tf_op jit(solution)/shard_map/all_to_all | solution.py:95
  84.7 0.2 reduce-scatter.4.cloned.1.call-start
  85.0 5.4 %fusion.11 = f32[512,704]{0,1:T(8,128)} fusion(bf16[512,2048]{1,0:T(8,128)(2,1)} %bitcast.3, bf16[1,2048,704]{1,2,0:T(8,128)(2,1)} %param.11), kind=kOutput, calls=%fused_computation.23 | convolution fusion | flops 1476395008 | bytes 6422528 | tf_op jit(solution)/shard_map/dot_general | solution.py:20
  90.4 4.4 %fusion.7 = f32[512,704]{0,1:T(8,128)} fusion(bf16[512,2048]{1,0:T(8,128)(2,1)} %bitcast.3, bf16[1,2048,704]{1,2,0:T(8,128)(2,1)S(1)} %copy-done.4), kind=kOutput, calls=%fused_computation.19 | convolution fusion | flops 1476395008 | bytes 6422528 | tf_op jit(solution)/shard_map/dot_general | solution.py:21
  94.7 37.8 %all-to-all-done.2 = bf16[8,64,2048]{2,1,0:T(8,128)(2,1)} async-done(((bf16[8,64,2048]{2,1,0:T(8,128)(2,1)}), bf16[8,64,2048]{2,1,0:T(8,128)(2,1)}, u32[]{:S(2)}, u32[]{:S(2)}) %all-to-all-start.2) | async-done | bytes 2097184 | tf_op jit(solution)/shard_map/all_to_all | solution.py:95
  132.6 5.7 %multiply_convert_fusion.2 = (bf16[512,704]{0,1:T(8,128)(2,1)}, bf16[512,704]{0,1:T(8,128)(2,1)S(1)}, bf16[512,704]{0,1:T(8,128)(2,1)}) fusion(f32[512,704]{0,1:T(8,128)} %fusion.11, f32[512,704]{0,1:T(8,128)} %fusion.7, bf16[512,2048]{1,0:T(8,128)(2,1)} %bitcast.10, bf16[1,704,2048]{2,1,0:T(8,128)(2,1)S(1)} %copy-done), kind=kOutput, calls=%fused_computation.27 | convolution fusion | flops 1482162176 | bytes 10027008 | tf_op jit(solution)/shard_map/dot_general | solution.py:8
  138.3 0.9 copy-done.2
  139.2 4.9 %fusion.1 = bf16[1,2048,704]{1,2,0:T(8,128)(2,1)} fusion(bf16[512,704]{0,1:T(8,128)(2,1)S(1)} %get-tuple-element.15, bf16[512,2048]{1,0:T(8,128)(2,1)} %bitcast.3), kind=kOutput, calls=%fused_computation.13 | convolution fusion | flops 1477836800 | bytes 5701632 | tf_op jit(solution)/shard_map/dot_general | solution.py:14
  144.1 5.1 %fusion.2 = bf16[1,2048,704]{1,2,0:T(8,128)(2,1)} fusion(bf16[512,704]{0,1:T(8,128)(2,1)} %get-tuple-element.14, bf16[512,2048]{1,0:T(8,128)(2,1)} %bitcast.3), kind=kOutput, calls=%fused_computation.14 | convolution fusion | flops 1477836800 | bytes 5701632 | tf_op jit(solution)/shard_map/dot_general | solution.py:14
  149.3 4.5 %fusion.9 = f32[512,2048]{1,0:T(8,128)S(1)} fusion(bf16[512,704]{0,1:T(8,128)(2,1)} %copy-done.2, bf16[1,2048,704]{1,2,0:T(8,128)(2,1)} %param.11), kind=kOutput, calls=%fused_computation.21 | convolution fusion | flops 1476395008 | bytes 7798784 | tf_op jit(solution)/shard_map/dot_general | solution.py:8
  153.8 3.3 %add_convert_fusion = bf16[512,2048]{1,0:T(8,128)(2,1)} fusion(f32[512,2048]{1,0:T(8,128)S(1)} %fusion.9, bf16[512,704]{0,1:T(8,128)(2,1)S(1)} %copy-done.6, bf16[1,2048,704]{1,2,0:T(8,128)(2,1)S(1)} %copy-done.5), kind=kOutput, calls=%fused_computation.4 | convolution fusion | flops 1478492160 | bytes 9895936 | tf_op jit(solution)/shard_map/dot_general | solution.py:8
  157.1 4.4 %all-to-all-start.3 = ((bf16[8,64,2048]{2,1,0:T(8,128)(2,1)}), bf16[8,64,2048]{2,1,0:T(8,128)(2,1)}, u32[]{:S(2)}, u32[]{:S(2)}) async-start(bf16[8,64,2048]{2,1,0:T(8,128)(2,1)} %bitcast.54), calls=%async_computation.3 | async-start | bytes 4194304 | tf_op jit(solution)/shard_map/all_to_all | solution.py:101
  161.5 0.3 reduce-scatter.8.cloned.1.call-start
  161.8 5.1 %fusion = bf16[1,704,2048]{2,1,0:T(8,128)(2,1)} fusion(bf16[512,704]{0,1:T(8,128)(2,1)} %get-tuple-element.16, bf16[512,2048]{1,0:T(8,128)(2,1)} %bitcast.10), kind=kOutput, calls=%fused_computation.12 | convolution fusion | flops 1477836800 | bytes 5701632 | tf_op jit(solution)/shard_map/dot_general | solution.py:14
  166.9 4.3 %convolution_convert_fusion.3 = bf16[512,2048]{1,0:T(8,128)(2,1)} fusion(bf16[512,704]{0,1:T(8,128)(2,1)} %get-tuple-element.16, bf16[1,704,2048]{2,1,0:T(8,128)(2,1)S(1)} %copy-done), kind=kOutput, calls=%fused_computation.11 | convolution fusion | flops 1477443584 | bytes 5701632 | tf_op jit(solution)/shard_map/dot_general | solution.py:23
  171.2 38.1 %all-to-all-done.3 = bf16[8,64,2048]{2,1,0:T(8,128)(2,1)} async-done(((bf16[8,64,2048]{2,1,0:T(8,128)(2,1)}), bf16[8,64,2048]{2,1,0:T(8,128)(2,1)}, u32[]{:S(2)}, u32[]{:S(2)}) %all-to-all-start.3) | async-done | bytes 2097184 | tf_op jit(solution)/shard_map/all_to_all | solution.py:101
  209.3 4.4 %all-to-all-start.1 = ((bf16[8,64,2048]{2,1,0:T(8,128)(2,1)}), bf16[8,64,2048]{2,1,0:T(8,128)(2,1)}, u32[]{:S(2)}, u32[]{:S(2)}) async-start(bf16[8,64,2048]{2,1,0:T(8,128)(2,1)} %bitcast.55), calls=%async_computation.1 | async-start | bytes 4194304 | tf_op jit(solution)/shard_map/all_to_all | solution.py:94
  213.6 1.1 convert_element_type.83
  214.7 7.0 %gather_fusion.1 = bf16[384,2048]{1,0:T(8,128)(2,1)} fusion(bf16[512,2048]{1,0:T(8,128)(2,1)} %bitcast.12, s32[1024]{0:T(1024)S(1)} %pad_clamp_fusion), kind=kCustom, calls=%fused_computation.1 | custom fusion | bytes 3147264 | tf_op jit(solution)/shard_map/gather | solution.py:75
  221.7 5.2 %reshape.120 = bf16[128,3,2048]{2,1,0:T(4,128)(2,1)} reshape(bf16[384,2048]{1,0:T(8,128)(2,1)} %gather_fusion.1) | data formatting | bytes 3145728 | tf_op jit(solution)/shard_map/reshape | solution.py:75
  226.8 5.0 %reduce_sum.45 = bf16[128,2048]{1,0:T(8,128)(2,1)} reduce(bf16[128,3,2048]{2,1,0:T(4,128)(2,1)} %reshape.120, bf16[]{:T(256)} %constant.6.clone.1), dimensions={1}, to_apply=%region_7.8 | reduce | flops 524288 | bytes 2097154 | tf_op jit(solution)/shard_map/reduce_sum | solution.py:107
  231.8 29.6 %all-to-all-done.1 = bf16[8,64,2048]{2,1,0:T(8,128)(2,1)} async-done(((bf16[8,64,2048]{2,1,0:T(8,128)(2,1)}), bf16[8,64,2048]{2,1,0:T(8,128)(2,1)}, u32[]{:S(2)}, u32[]{:S(2)}) %all-to-all-start.1) | async-done | bytes 2097184 | tf_op jit(solution)/shard_map/all_to_all | solution.py:94
  261.4 6.9 %gather_fusion = bf16[384,2048]{1,0:T(8,128)(2,1)} fusion(bf16[512,2048]{1,0:T(8,128)(2,1)} %bitcast.8, s32[1024]{0:T(1024)S(1)} %pad_clamp_fusion), kind=kCustom, calls=%fused_computation | custom fusion | bytes 3147264 | tf_op jit(solution)/shard_map/gather | solution.py:75
  268.4 5.5 %reshape.121 = f32[128,3,2048]{2,1,0:T(4,128)} reshape(bf16[384,2048]{1,0:T(8,128)(2,1)} %gather_fusion) | data formatting | bytes 4718592 | tf_op jit(solution)/shard_map/convert_element_type | solution.py:104
  273.8 6.6 %multiply_reduce_fusion = (f32[128,3]{1,0:T(8,128)S(1)}, bf16[128,2048]{1,0:T(8,128)(2,1)}) fusion(f32[128,3,2048]{2,1,0:T(4,128)} %reshape.121, f32[128,2048]{1,0:T(8,128)} %convert_element_type.83, f32[128,3]{1,0:T(8,128)S(1)} %copy.19), kind=kLoop, calls=%fused_computation.5 | loop fusion | flops 2883200 | bytes 4721664 | tf_op jit(solution)/shard_map/reduce_sum | solution.py:106
  280.5 0.7 copy.24
  281.1 2.4 convert_element_type.91
  283.5 2.4 convert_element_type.94
  285.9 2.4 convert_element_type.97
  (24 shorter events, 0.2 us)
Async XLA Ops:
  7.2 125.4 %copy-start = (bf16[1,704,2048]{2,1,0:T(8,128)(2,1)S(1)}, bf16[1,704,2048]{2,1,0:T(8,128)(2,1)}, u32[]{:S(2)}) copy-start(bf16[1,704,2048]{2,1,0:T(8,128)(2,1)} %param.13) | copy-start | bytes 8650756
  24.6 7.4 %copy-start.3 = (f32[128,3]{0,1:T(4,128)S(1)}, f32[128,3]{0,1:T(4,128)}, u32[]{:S(2)}) copy-start(f32[128,3]{0,1:T(4,128)} %param.10) | copy-start | bytes 4612
  24.6 7.7 %copy-start.1 = (bf16[128,2048]{1,0:T(8,128)(2,1)S(1)}, bf16[128,2048]{1,0:T(8,128)(2,1)}, u32[]{:S(2)}) copy-start(bf16[128,2048]{1,0:T(8,128)(2,1)} %param.8) | copy-start | bytes 1572868
  24.6 55.8 %all-to-all-start = ((bf16[8,64,2048]{2,1,0:T(8,128)(2,1)}), bf16[8,64,2048]{2,1,0:T(8,128)(2,1)}, u32[]{:S(2)}, u32[]{:S(2)}) async-start(bf16[8,64,2048]{2,1,0:T(8,128)(2,1)} %bitcast.53), calls=%async_computation | async-start | bytes 4194304 | tf_op jit(solution)/shard_map/all_to_all | solution.py:90
  80.4 52.2 %all-to-all-start.2 = ((bf16[8,64,2048]{2,1,0:T(8,128)(2,1)}), bf16[8,64,2048]{2,1,0:T(8,128)(2,1)}, u32[]{:S(2)}, u32[]{:S(2)}) async-start(bf16[8,64,2048]{2,1,0:T(8,128)(2,1)} %bitcast.52), calls=%async_computation.2 | async-start | bytes 4194304 | tf_op jit(solution)/shard_map/all_to_all | solution.py:95
  84.7 196.4 %reduce-scatter.4.cloned.1.call-start = ((), (), s32[]{:S(2)}) async-start(), calls=%async_computation.7 | async-start | bytes 3604480 | tf_op jit(solution)/shard_map/reduce_scatter | solution.py:109
  85.0 5.4 %copy-start.4 = (bf16[1,2048,704]{1,2,0:T(8,128)(2,1)S(1)}, bf16[1,2048,704]{1,2,0:T(8,128)(2,1)}, u32[]{:S(2)}) copy-start(bf16[1,2048,704]{1,2,0:T(8,128)(2,1)} %param.12) | copy-start | bytes 8650756
  138.3 0.9 copy-start.2
  144.1 139.5 %reduce-scatter.6.cloned.1.call-start = ((), (), s32[]{:S(2)}) async-start(), calls=%async_computation.8 | async-start | bytes 3604480 | tf_op jit(solution)/shard_map/reduce_scatter | solution.py:112
  149.3 4.5 %copy-start.5 = (bf16[1,2048,704]{1,2,0:T(8,128)(2,1)S(1)}, bf16[1,2048,704]{1,2,0:T(8,128)(2,1)}, u32[]{:S(2)}) copy-start(bf16[1,2048,704]{1,2,0:T(8,128)(2,1)} %param.12) | copy-start | bytes 8650756
  149.3 4.5 %copy-start.6 = (bf16[512,704]{0,1:T(8,128)(2,1)S(1)}, bf16[512,704]{0,1:T(8,128)(2,1)}, u32[]{:S(2)}) copy-start(bf16[512,704]{0,1:T(8,128)(2,1)} %get-tuple-element.14) | copy-start | bytes 2162692
  157.1 52.1 %all-to-all-start.3 = ((bf16[8,64,2048]{2,1,0:T(8,128)(2,1)}), bf16[8,64,2048]{2,1,0:T(8,128)(2,1)}, u32[]{:S(2)}, u32[]{:S(2)}) async-start(bf16[8,64,2048]{2,1,0:T(8,128)(2,1)} %bitcast.54), calls=%async_computation.3 | async-start | bytes 4194304 | tf_op jit(solution)/shard_map/all_to_all | solution.py:101
  161.5 124.4 %reduce-scatter.8.cloned.1.call-start = ((), (), s32[]{:S(2)}) async-start(), calls=%async_computation.9 | async-start | bytes 3604480 | tf_op jit(solution)/shard_map/reduce_scatter | solution.py:115
  209.3 52.2 %all-to-all-start.1 = ((bf16[8,64,2048]{2,1,0:T(8,128)(2,1)}), bf16[8,64,2048]{2,1,0:T(8,128)(2,1)}, u32[]{:S(2)}, u32[]{:S(2)}) async-start(bf16[8,64,2048]{2,1,0:T(8,128)(2,1)} %bitcast.55), calls=%async_computation.1 | async-start | bytes 4194304 | tf_op jit(solution)/shard_map/all_to_all | solution.py:94
Sparse Core Ops, SparseCore 0:
  144.2 35.3 reduce-scatter.3
  182.3 36.3 reduce-scatter.5
  221.2 36.3 reduce-scatter.7
where the time goes:
time: 296 us; the launch traced here: 295 us
  waiting for transfers between devices  139 us (47%)
  local copies, waits for them, and re-layouts  51.1 us (17%)
  matrix products  42.7 us (14%)
  other arithmetic  27.4 us (9%)
  starting transfers between devices  21 us (7%)
  between operations  13.9 us (5%)
    all_to_all x1, waiting for transfers between devices, shards(): lax.all_to_all(unflatten(route_grad), 'expert', split_axis=0, concat_axis...  38.1 us
    all_to_all x1, waiting for transfers between devices, shards(): lax.all_to_all(dispatch(out_grad), 'expert', split_axis=0, concat_axis=0,...  37.8 us
    all_to_all x1, waiting for transfers between devices, shards(): lax.all_to_all(dispatch(token_copies), 'expert', split_axis=0, concat_axi...  33.3 us
    all_to_all x1, waiting for transfers between devices, shards(): lax.all_to_all(unflatten(result), 'expert', split_axis=0, concat_axis=0,...  29.6 us
    dot_general x3, matrix products, contract_rows(): lax.dot_general(left, right, (((0,), (0,)), ((), ())), preferred_element_...  15.1 us
    gather x2, local copies, waits for them, and re-layouts, collect(): buffer.reshape(slots_total, model_width)[target]  13.9 us
    dot_general x3, matrix products, contract_last(): lax.dot_general(left, right, (((1,), (1,)), ((), ())), preferred_element_...  13.6 us
    all_to_all x1, starting transfers between devices, shards(): lax.all_to_all(dispatch(token_copies), 'expert', split_axis=0, concat_axi...  7.41 us
  transfers between devices with their start and end apart: 7, of which 4 were waited for; matrix products, arithmetic and copies ran while one was open for 30% of the time, Pallas kernels for 0%

commit v1 on v0

v1 whole, which is shorter than its diff:
```python
import jax
import jax.numpy as jnp
from jax import lax
from jax.sharding import PartitionSpec as P

F32 = jnp.float32
BF16 = jnp.bfloat16


def dot(left, right, dims):
    return lax.dot_general(left, right, (dims, ((), ())), preferred_element_type=F32)


def shards(tokens, upstream, expert_ids, gate_probs, w_gate, w_up, w_down):
    tok_rows, width = tokens.shape
    routes = expert_ids.shape[1]
    experts = lax.axis_size("expert")
    capacity = 4 * tok_rows * routes // (3 * experts)
    w_gate, w_up, w_down = w_gate[0], w_up[0], w_down[0]

    picks = expert_ids[None] == jnp.arange(experts, dtype=jnp.int32)[:, None, None]
    dense = jnp.sum(jnp.where(picks, gate_probs[None], 0.0), axis=2)
    dense = jnp.where(jnp.any(picks, axis=2), dense, -1.0)
    probs = lax.all_to_all(dense, "expert", split_axis=0, concat_axis=0, tiled=True)

    all_tokens = lax.all_gather(tokens, "expert")
    all_upstream = lax.all_gather(upstream, "expert")

    routed = probs >= 0.0
    counts = routed.astype(jnp.int32)
    slot = jnp.cumsum(counts, axis=1) - counts
    chosen = routed[:, None, :] & (
        slot[:, None, :] == jnp.arange(capacity, dtype=jnp.int32)[None, :, None]
    )
    select = chosen.astype(BF16)
    row_probs = jnp.sum(jnp.where(chosen, probs[:, None, :], 0.0), axis=2).reshape(-1, 1)

    def pick(values):
        return (
            jnp.einsum("bct,btd->bcd", select, values, preferred_element_type=F32)
            .astype(BF16)
            .reshape(experts * capacity, width)
        )

    def spread(rows):
        rows = rows.reshape(experts, capacity, width)
        return jnp.einsum("bct,bcd->btd", select, rows, preferred_element_type=F32).astype(BF16)

    rows = pick(all_tokens)
    gate_pre = dot(rows, w_gate, ((1,), (0,)))
    up_pre = dot(rows, w_up, ((1,), (0,)))
    sig = jax.nn.sigmoid(gate_pre)
    hidden = (gate_pre * sig * up_pre).astype(BF16)
    weighted = (dot(hidden, w_down, ((1,), (0,))) * row_probs).astype(BF16)
    mixed = lax.psum_scatter(spread(weighted), "expert", scatter_dimension=0)

    grads = pick(all_upstream)
    raw = dot(grads, w_down, ((1,), (1,)))
    row_dots = jnp.sum(raw * hidden.astype(F32), axis=1).reshape(experts, capacity, 1)
    hidden_grad = raw * row_probs
    gate_grad = (hidden_grad * up_pre * sig * (1.0 + gate_pre * (1.0 - sig))).astype(BF16)
    up_grad = (hidden_grad * gate_pre * sig).astype(BF16)
    scaled_hidden = (hidden.astype(F32) * row_probs).astype(BF16)
    route_grad = (
        dot(gate_grad, w_gate, ((1,), (1,))) + dot(up_grad, w_up, ((1,), (1,)))
    ).astype(BF16)
    token_grad = lax.psum_scatter(spread(route_grad), "expert", scatter_dimension=0)

    token_dots = jnp.sum(jnp.where(chosen, row_dots, 0.0), axis=1)
    back = lax.all_to_all(token_dots, "expert", split_axis=0, concat_axis=0, tiled=True)
    grad_probs = jnp.sum(jnp.where(picks, back[:, :, None], 0.0), axis=0)

    def scatter(partial, dim):
        return lax.psum_scatter(
            partial[None].astype(BF16), "dp", scatter_dimension=dim, tiled=True
        ).astype(F32)

    grad_gate = scatter(dot(rows, gate_grad, ((0,), (0,))), 1)
    grad_up = scatter(dot(rows, up_grad, ((0,), (0,))), 1)
    grad_down = scatter(dot(scaled_hidden, grads, ((0,), (0,))), 2)
    return (mixed, grad_probs, token_grad, grad_gate, grad_up, grad_down)


def solution(mesh):
    rows = P(("dp", "expert"), None)
    weights = P("expert", None, None)
    return jax.shard_map(
        shards,
        mesh=mesh,
        in_specs=(rows, rows, rows, rows, weights, weights, weights),
        out_specs=(
            rows,
            rows,
            rows,
            P("expert", "dp", None),
            P("expert", "dp", None),
            P("expert", None, "dp"),
        ),
        check_vma=False,
    )
```

time: 296 us -> 481 us (1.62)
  waiting for transfers between devices: 139 us -> 383 us
  local copies, waits for them, and re-layouts: 51.1 us -> 2.26 us
  blocking collectives: 0 us -> 23.1 us
  starting transfers between devices: 21 us -> 0.46 us
  other arithmetic: 27.4 us -> 13.6 us
    reduce_scatter x3 -> x5, waiting for transfers between devices: 0.01 us -> 250 us  [the longest x1 91.9 us: shards(): lax.psum_scatter(spread(route_grad), 'expert', scatter_dimension=0)]
    all_to_all x4 -> x0, waiting for transfers between devices: 139 us -> none  [the longest x1 38.1 us: shards(): lax.all_to_all(unflatten(route_grad), 'expert', split_axis=0, concat_axis...]
    all_gather x0 -> x2, waiting for transfers between devices: none -> 132 us  [the longest x1 69.5 us: shards(): all_tokens = lax.all_gather(tokens, 'expert')]
    all_to_all x0 -> x2, blocking collectives: none -> 23.1 us  [the longest x1 13.5 us: shards(): lax.all_to_all(dense, 'expert', split_axis=0, concat_axis=0, tiled=True)]
    all_to_all x4 -> x0, starting transfers between devices: 20.5 us -> none  [the longest x1 7.41 us: shards(): lax.all_to_all(dispatch(token_copies), 'expert', split_axis=0, concat_axi...]
    gather x2 -> x0, local copies, waits for them, and re-layouts: 13.9 us -> none  [collect(): buffer.reshape(slots_total, model_width)[target]]
    convert_element_type x2 -> x0, local copies, waits for them, and re-layouts: 11.4 us -> none  [the longest x1 5.96 us: shards(): jnp.repeat(upstream, routes, axis=0).astype(jnp.float32)]
    reshape x2 -> x0, local copies, waits for them, and re-layouts: 10.2 us -> none  [the longest x1 5.17 us: collect(): buffer.reshape(slots_total, model_width)[target]]
  transfers between devices with their start and end apart: 7 -> 7, of which waited for: 4 -> 6; matrix products, arithmetic and copies ran while one was open for 30% -> 9% of each run, Pallas kernels for 0% -> 0%
where the time goes in v1:
time: 481 us; the launch traced here: 480 us
  waiting for transfers between devices  383 us (80%)
  matrix products  43 us (9%)
  blocking collectives  23.1 us (5%)
  between operations  14.3 us (3%)
  other arithmetic  13.6 us (3%)
    reduce_scatter x1, waiting for transfers between devices, shards(): lax.psum_scatter(spread(route_grad), 'expert', scatter_dimension=0)  91.9 us
    reduce_scatter x1, waiting for transfers between devices, shards(): mixed = lax.psum_scatter(spread(weighted), 'expert', scatter_dimension=0)  90 us
    all_gather x1, waiting for transfers between devices, shards(): all_tokens = lax.all_gather(tokens, 'expert')  69.5 us
    reduce_scatter x3, waiting for transfers between devices, scatter(): lax.psum_scatter(partial[None].astype(BF16), 'dp', scatter_dimension=dim,...  68.2 us
    all_gather x1, waiting for transfers between devices, shards(): all_upstream = lax.all_gather(upstream, 'expert')  62.3 us
    dot_general x9, matrix products, dot(): lax.dot_general(left, right, (dims, ((), ())), preferred_element_type=F32)  29.2 us
    all_to_all x1, blocking collectives, shards(): lax.all_to_all(dense, 'expert', split_axis=0, concat_axis=0, tiled=True)  13.5 us
  transfers between devices with their start and end apart: 7, of which 6 were waited for; matrix products, arithmetic and copies ran while one was open for 9% of the time, Pallas kernels for 0%

profile of v1, /device:TPU:0, one launch (start us, length us, event | category | flops | bytes accessed | tf_op | source)
XLA Modules:
  0.0 480.2 jit_solution(5930573305243820109)
XLA Ops:
  7.2 0.0 all-gather.7.cloned.1.call-start
  7.2 0.7 all-gather.7.cloned.1.call-update
  7.9 0.0 all-gather.5.cloned.1.call-start
  8.0 0.7 all-gather.5.cloned.1.call-update
  8.7 0.0 reduce-scatter.14.cloned.1.call-start
  8.7 0.7 fusion.30
  9.4 0.7 select_reduce_fusion.3
  10.1 13.5 %all_to_all.18 = f32[8,1,128]{2,1,0:T(1,128)S(1)} all-to-all(f32[8,1,128]{2,1,0:T(1,128)S(1)} %bitcast.73), channel_id=1, replica_groups=mesh['dp'=4,'expert'=8] {'expert'}, dimensions={0} | all-to-all | bytes 8192 | tf_op jit(solution)/shard_map/all_to_all | solution.py:24
  23.7 0.3 reduce_window_sum.11
  24.0 62.3 %all-gather.7.cloned.1.call-done = bf16[1024,2048]{1,0:T(8,128)(2,1)} async-done(((bf16[128,2048]{1,0:T(8,128)(2,1)}), bf16[1024,2048]{1,0:T(8,128)(2,1)}) %all-gather.7.cloned.1.call-update) | async-done | bytes 4194320 | tf_op jit(solution)/shard_map/all_gather | solution.py:27
  86.3 4.3 convolution_convert_fusion.5
  90.6 69.5 %all-gather.5.cloned.1.call-done = bf16[1024,2048]{1,0:T(8,128)(2,1)} async-done(((bf16[128,2048]{1,0:T(8,128)(2,1)}), bf16[1024,2048]{1,0:T(8,128)(2,1)}) %all-gather.5.cloned.1.call-update) | async-done | bytes 4194320 | tf_op jit(solution)/shard_map/all_gather | solution.py:26
  160.1 3.0 convolution_convert_fusion.6
  163.1 0.0 copy-done.10
  163.2 1.7 fusion.7
  164.9 0.9 copy-done.1
  165.7 1.8 fusion.11
  167.5 0.3 copy-done.4
  167.8 3.2 fusion.13
  171.1 0.1 broadcast_in_dim.68
  171.1 0.2 select_reduce_fusion
  171.4 0.1 mul.53
  171.5 5.1 %fusion = bf16[1,704,2048]{2,1,0:T(8,128)(2,1)} fusion(bf16[512,2048]{1,0:T(8,128)(2,1)} %bitcast.62, bf16[512,704]{0,1:T(8,128)(2,1)} %get-tuple-element.9, f32[512]{0:T(512)S(1)} %mul.53), kind=kOutput, calls=%fused_computation.9 | convolution fusion | flops 1478918144 | bytes 5703680 | tf_op jit(solution)/shard_map/dot_general | solution.py:11
  176.6 0.0 reduce-scatter.14.cloned.1.call-update
  176.6 0.0 reduce-scatter.12.cloned.1.call-start
  176.7 3.9 multiply_convert_fusion.1
  180.6 0.9 copy-done.7
  181.4 3.2 fusion.2
  184.7 0.0 reduce-scatter.10.cloned.1.call-start
  184.7 5.2 %fusion.1 = bf16[1,2048,704]{1,2,0:T(8,128)(2,1)} fusion(bf16[512,704]{0,1:T(8,128)(2,1)} %get-tuple-element.13, bf16[512,2048]{1,0:T(8,128)(2,1)} %bitcast.60), kind=kOutput, calls=%fused_computation.10 | convolution fusion | flops 1477836800 | bytes 5701632 | tf_op jit(solution)/shard_map/dot_general | solution.py:11
  190.0 0.0 reduce-scatter.10.cloned.1.call-update
  190.0 0.2 reduce-scatter.6.cloned.1.call-start
  190.2 2.9 multiply_convert_fusion
  193.2 3.2 convolution_convert_fusion.1
  196.4 0.0 reduce-scatter.6.cloned.1.call-update
  196.4 0.0 reduce-scatter.8.cloned.1.call-start
  196.5 4.0 fusion.9
  200.6 2.0 add_convert_fusion
  202.6 3.3 convolution_convert_fusion
  205.8 9.6 %all_to_all.19 = f32[8,1,128]{2,1,0:T(1,128)S(1)} all-to-all(f32[8,1,128]{2,1,0:T(1,128)S(1)} %bitcast.75), channel_id=1, replica_groups=mesh['dp'=4,'expert'=8] {'expert'}, dimensions={0} | all-to-all | bytes 8192 | tf_op jit(solution)/shard_map/all_to_all | solution.py:70
  215.4 0.6 select_reduce_fusion.2
  216.0 2.4 convert_element_type.87
  218.4 31.9 %reduce-scatter.12.cloned.1.call-done = bf16[1,512,704]{1,2,0:T(8,128)(2,1)} async-done(((bf16[1,2048,704]{1,2,0:T(8,128)(2,1)}), bf16[1,512,704]{1,2,0:T(8,128)(2,1)}) %reduce-scatter.12.cloned.1.call-update) | async-done | bytes 720912 | tf_op jit(solution)/shard_map/reduce_scatter | solution.py:74
  250.3 2.4 convert_element_type.83
  252.7 36.3 %reduce-scatter.10.cloned.1.call-done = bf16[1,512,704]{1,2,0:T(8,128)(2,1)} async-done(((bf16[1,2048,704]{1,2,0:T(8,128)(2,1)}), bf16[1,512,704]{1,2,0:T(8,128)(2,1)}) %reduce-scatter.10.cloned.1.call-update) | async-done | bytes 720912 | tf_op jit(solution)/shard_map/reduce_scatter | solution.py:74
  289.0 2.4 convert_element_type.80
  291.4 90.0 %reduce-scatter.6.cloned.1.call-done = bf16[1,128,2048]{2,1,0:T(8,128)(2,1)} async-done(((bf16[8,128,2048]{2,1,0:T(8,128)(2,1)}), bf16[1,128,2048]{2,1,0:T(8,128)(2,1)}) %reduce-scatter.6.cloned.1.call-update) | async-done | bytes 524304 | tf_op jit(solution)/shard_map/reduce_scatter | solution.py:55
  381.5 91.9 %reduce-scatter.8.cloned.1.call-done = bf16[1,128,2048]{2,1,0:T(8,128)(2,1)} async-done(((bf16[8,128,2048]{2,1,0:T(8,128)(2,1)}), bf16[1,128,2048]{2,1,0:T(8,128)(2,1)}) %reduce-scatter.8.cloned.1.call-update) | async-done | bytes 524304 | tf_op jit(solution)/shard_map/reduce_scatter | solution.py:67
  (26 shorter events, 0.1 us)
Async XLA Ops:
  7.2 160.4 %copy-start = (bf16[1,704,2048]{2,1,0:T(8,128)(2,1)S(1)}, bf16[1,704,2048]{2,1,0:T(8,128)(2,1)}, u32[]{:S(2)}) copy-start(bf16[1,704,2048]{2,1,0:T(8,128)(2,1)} %param.13) | copy-start | bytes 8650756
  7.2 79.1 %all-gather.7.cloned.1.call-start = ((), (), s32[]{:S(2)}) async-start(), calls=%async_computation.13 | async-start | bytes 4718592 | tf_op jit(solution)/shard_map/all_gather | solution.py:27
  7.9 152.2 %all-gather.5.cloned.1.call-start = ((), (), s32[]{:S(2)}) async-start(), calls=%async_computation.12 | async-start | bytes 4718592 | tf_op jit(solution)/shard_map/all_gather | solution.py:26
  8.7 207.4 %reduce-scatter.14.cloned.1.call-start = ((), (), s32[]{:S(2)}) async-start(), calls=%async_computation.11 | async-start | bytes 3604480 | tf_op jit(solution)/shard_map/reduce_scatter | solution.py:74
  160.1 3.1 copy-start.10
  163.1 1.7 copy-start.2
  163.2 2.6 copy-start.1
  165.7 1.8 copy-start.5
  165.7 2.1 copy-start.4
  167.5 3.6 copy-start.6
  176.6 73.7 %reduce-scatter.12.cloned.1.call-start = ((), (), s32[]{:S(2)}) async-start(), calls=%async_computation.10 | async-start | bytes 3604480 | tf_op jit(solution)/shard_map/reduce_scatter | solution.py:74
  176.7 4.8 copy-start.3
  180.6 0.9 copy-start.7
  184.7 104.4 %reduce-scatter.10.cloned.1.call-start = ((), (), s32[]{:S(2)}) async-start(), calls=%async_computation.9 | async-start | bytes 3604480 | tf_op jit(solution)/shard_map/reduce_scatter | solution.py:74
  190.0 191.5 %reduce-scatter.6.cloned.1.call-start = ((), (), s32[]{:S(2)}) async-start(), calls=%async_computation.7 | async-start | bytes 4718592 | tf_op jit(solution)/shard_map/reduce_scatter | solution.py:55
  196.4 276.9 %reduce-scatter.8.cloned.1.call-start = ((), (), s32[]{:S(2)}) async-start(), calls=%async_computation.8 | async-start | bytes 4718592 | tf_op jit(solution)/shard_map/reduce_scatter | solution.py:67
  196.5 4.1 copy-start.8
  196.5 4.1 copy-start.11
  205.8 9.6 %copy-start.9 = (s32[128,3]{0,1:T(4,128)S(1)}, s32[128,3]{0,1:T(4,128)}, u32[]{:S(2)}) copy-start(s32[128,3]{0,1:T(4,128)} %param.9) | copy-start | bytes 4612
Sparse Core Ops, SparseCore 0:
  10.1 76.0 all-gather.6
  88.4 71.6 all-gather.4
  176.7 34.5 reduce-scatter.13
  213.9 36.3 reduce-scatter.11
  252.7 36.3 reduce-scatter.9
  293.5 87.8 reduce-scatter.5
  385.7 87.6 reduce-scatter.7

commit v2 on v1

v2 whole, which is shorter than its diff:
```python
import jax
import jax.numpy as jnp
from jax import lax
from jax.sharding import PartitionSpec as P

F32 = jnp.float32
BF16 = jnp.bfloat16


def dot(left, right, dims):
    return lax.dot_general(left, right, (dims, ((), ())), preferred_element_type=F32)


def shards(tokens, upstream, expert_ids, gate_probs, w_gate, w_up, w_down):
    tok_rows, width = tokens.shape
    routes = expert_ids.shape[1]
    experts = lax.axis_size("expert")
    capacity = 4 * tok_rows * routes // (3 * experts)
    w_gate, w_up, w_down = w_gate[0], w_up[0], w_down[0]

    ids = jnp.transpose(expert_ids)
    picks = ids[None] == jnp.arange(experts, dtype=jnp.int32)[:, None, None]
    routed = jnp.any(picks, axis=1)
    dense = jnp.sum(jnp.where(picks, jnp.transpose(gate_probs)[None], 0.0), axis=1)
    counts = routed.astype(F32)
    earlier = jnp.arange(tok_rows)[:, None] < jnp.arange(tok_rows)[None, :]
    slot = dot(counts.astype(BF16), earlier.astype(BF16), ((1,), (0,))).astype(jnp.int32)
    chosen = routed[:, None, :] & (
        slot[:, None, :] == jnp.arange(capacity, dtype=jnp.int32)[None, :, None]
    )
    select = chosen.astype(BF16).reshape(experts * capacity, tok_rows)
    send_probs = jnp.sum(jnp.where(chosen, dense[:, None, :], 0.0), axis=2)

    def exchange(values):
        return lax.all_to_all(
            values.reshape(experts, capacity, -1), "expert", split_axis=0, concat_axis=0, tiled=True
        ).reshape(experts * capacity, -1)

    rows = exchange(dot(select, tokens, ((1,), (0,))).astype(BF16))
    out_grad = dot(select, upstream, ((1,), (0,))) * send_probs.reshape(-1, 1)
    grads = exchange(out_grad.astype(BF16))

    gate_pre = dot(rows, w_gate, ((1,), (0,)))
    up_pre = dot(rows, w_up, ((1,), (0,)))
    sig = jax.nn.sigmoid(gate_pre)
    hidden = (gate_pre * sig * up_pre).astype(BF16)
    result = dot(hidden, w_down, ((1,), (0,))).astype(BF16)
    back_out = exchange(result)

    hidden_grad = dot(grads, w_down, ((1,), (1,)))
    gate_grad = (hidden_grad * up_pre * sig * (1.0 + gate_pre * (1.0 - sig))).astype(BF16)
    up_grad = (hidden_grad * gate_pre * sig).astype(BF16)

    def scatter(partial, dim):
        partial = partial[None].astype(BF16)
        return lax.psum_scatter(partial, "dp", scatter_dimension=dim, tiled=True).astype(F32)

    grad_gate = scatter(dot(rows, gate_grad, ((0,), (0,))), 1)
    grad_up = scatter(dot(rows, up_grad, ((0,), (0,))), 1)
    grad_down = scatter(dot(hidden, grads, ((0,), (0,))), 2)
    route_grad = (
        dot(gate_grad, w_gate, ((1,), (1,))) + dot(up_grad, w_up, ((1,), (1,)))
    ).astype(BF16)
    back_grad = exchange(route_grad)

    sent_up = dot(select, upstream, ((1,), (0,)))
    mixed_rows = (back_out.astype(F32) * send_probs.reshape(-1, 1)).astype(BF16)
    mixed = dot(select, mixed_rows, ((0,), (0,))).astype(BF16)
    row_dots = jnp.sum(sent_up * back_out.astype(F32), axis=1).reshape(experts, capacity, 1)
    token_dots = jnp.sum(jnp.where(chosen, row_dots, 0.0), axis=1)
    grad_probs = jnp.transpose(jnp.sum(jnp.where(picks, token_dots[:, None, :], 0.0), axis=0))
    token_grad = dot(select, back_grad, ((0,), (0,))).astype(BF16)
    return (mixed, grad_probs, token_grad, grad_gate, grad_up, grad_down)


def solution(mesh):
    rows = P(("dp", "expert"), None)
    weights = P("expert", None, None)
    return jax.shard_map(
        shards,
        mesh=mesh,
        in_specs=(rows, rows, rows, rows, weights, weights, weights),
        out_specs=(
            rows,
            rows,
            rows,
            P("expert", "dp", None),
            P("expert", "dp", None),
            P("expert", None, "dp"),
        ),
        check_vma=False,
    )
```

time: 481 us -> 313 us (0.65)
  waiting for transfers between devices: 383 us -> 122 us
  blocking collectives: 23.1 us -> 108 us
  starting transfers between devices: 0.46 us -> 9.15 us
    reduce_scatter x5 -> x3, waiting for transfers between devices: 250 us -> 31.4 us  [scatter(): lax.psum_scatter(partial, 'dp', scatter_dimension=dim, tiled=True)]
    all_gather x2 -> x0, waiting for transfers between devices: 132 us -> none  [the longest x1 69.5 us: shards(): all_tokens = lax.all_gather(tokens, 'expert')]
    all_to_all x0 -> x2, waiting for transfers between devices: none -> 90.8 us  [exchange(): lax.all_to_all(values.reshape(experts, capacity, -1), 'expert', split_axi...]
    all_to_all x2, blocking collectives: 23.1 us -> 108 us  [exchange(): lax.all_to_all(values.reshape(experts, capacity, -1), 'expert', split_axi...]
    dot_general x9 -> x14, matrix products: 29.2 us -> 44.6 us  [dot(): lax.dot_general(left, right, (dims, ((), ())), preferred_element_type=F32)]
    dot_general x4 -> x0, matrix products: 13.8 us -> none  [the longest x2 7.33 us: pick(): jnp.einsum('bct,btd->bcd', select, values, preferred_element_type=F32)]
    all_to_all x0 -> x2, starting transfers between devices: none -> 8.84 us  [exchange(): lax.all_to_all(values.reshape(experts, capacity, -1), 'expert', split_axi...]
    convert_element_type x5 -> x4, other arithmetic: 11.1 us -> 9.69 us  [the longest x3 7.22 us: scatter(): lax.psum_scatter(partial, 'dp', scatter_dimension=dim, tiled=True)]
  transfers between devices with their start and end apart: 7 -> 5, of which waited for: 6 -> 3; matrix products, arithmetic and copies ran while one was open for 9% -> 11% of each run, Pallas kernels for 0% -> 0%
where the time goes in v2:
time: 313 us; the launch traced here: 312 us
  waiting for transfers between devices  122 us (39%)
  blocking collectives  108 us (35%)
  matrix products  44.6 us (14%)
  between operations  13.9 us (4%)
  other arithmetic  11.5 us (4%)
  starting transfers between devices  9.15 us (3%)
  local copies, waits for them, and re-layouts  3.37 us (1%)
    all_to_all x2, blocking collectives, exchange(): lax.all_to_all(values.reshape(experts, capacity, -1), 'expert', split_axi...  108 us
    all_to_all x2, waiting for transfers between devices, exchange(): lax.all_to_all(values.reshape(experts, capacity, -1), 'expert', split_axi...  90.8 us
    dot_general x14, matrix products, dot(): lax.dot_general(left, right, (dims, ((), ())), preferred_element_type=F32)  44.6 us
    reduce_scatter x3, waiting for transfers between devices, scatter(): lax.psum_scatter(partial, 'dp', scatter_dimension=dim, tiled=True)  31.4 us
    all_to_all x2, starting transfers between devices, exchange(): lax.all_to_all(values.reshape(experts, capacity, -1), 'expert', split_axi...  8.84 us
    convert_element_type x3, other arithmetic, scatter(): lax.psum_scatter(partial, 'dp', scatter_dimension=dim, tiled=True)  7.22 us
  transfers between devices with their start and end apart: 5, of which 3 were waited for; matrix products, arithmetic and copies ran while one was open for 11% of the time, Pallas kernels for 0%

profile of v2, /device:TPU:0, one launch (start us, length us, event | category | flops | bytes accessed | tf_op | source)
XLA Modules:
  0.0 312.3 jit_solution(14864287741545281677)
XLA Ops:
  7.2 0.0 copy-start
  7.2 0.8 fusion.26
  8.0 0.1 convolution_convert_fusion.5
  8.2 0.1 eq.46
  8.2 0.1 fusion.21
  8.4 1.7 convolution_convert_fusion.4
  10.1 0.0 copy-start.1
  10.1 55.6 %all_to_all.20 = bf16[8,64,2048]{2,1,0:T(8,128)(2,1)S(1)} all-to-all(bf16[8,64,2048]{2,1,0:T(8,128)(2,1)S(1)} %bitcast.70), channel_id=1, replica_groups=mesh['dp'=4,'expert'=8] {'expert'}, dimensions={0} | all-to-all | bytes 4194304 | tf_op jit(solution)/shard_map/all_to_all | solution.py:35
  65.7 0.0 copy-done.1
  65.7 1.7 fusion.12
  67.4 0.0 copy-done.2
  67.4 0.9 copy-done.8
  68.3 2.9 multiply_convert_fusion.5
  71.2 3.2 %convolution_convert_fusion.3 = bf16[512,2048]{1,0:T(8,128)(2,1)} fusion(bf16[512,704]{0,1:T(8,128)(2,1)S(1)} %get-tuple-element.10, bf16[1,704,2048]{2,1,0:T(8,128)(2,1)S(1)} %copy-done), kind=kOutput, calls=%fused_computation.8 | convolution fusion | flops 1477443584 | bytes 5701632 | tf_op jit(solution)/shard_map/dot_general | solution.py:11
  74.4 4.5 %all-to-all-start.1 = ((bf16[8,64,2048]{2,1,0:T(8,128)(2,1)}), bf16[8,64,2048]{2,1,0:T(8,128)(2,1)}, u32[]{:S(2)}, u32[]{:S(2)}) async-start(bf16[8,64,2048]{2,1,0:T(8,128)(2,1)} %bitcast.78), calls=%async_computation.1 | async-start | bytes 4194304 | tf_op jit(solution)/shard_map/all_to_all | solution.py:35
  78.9 0.0 reduce-scatter.8.cloned.1.call-start
  79.0 47.3 %all-to-all-done.1 = bf16[8,64,2048]{2,1,0:T(8,128)(2,1)} async-done(((bf16[8,64,2048]{2,1,0:T(8,128)(2,1)}), bf16[8,64,2048]{2,1,0:T(8,128)(2,1)}, u32[]{:S(2)}, u32[]{:S(2)}) %all-to-all-start.1) | async-done | bytes 2097184 | tf_op jit(solution)/shard_map/all_to_all | solution.py:35
  126.3 4.2 %fusion = (f32[512]{0:T(512)S(1)}, f32[512,2048]{1,0:T(8,128)}) fusion(bf16[8,64,2048]{2,1,0:T(8,128)(2,1)} %all-to-all-done.1, pred[512,128]{1,0:T(32,128)(4,1)S(1)} %fusion.21, bf16[128,2048]{1,0:T(8,128)(2,1)S(1)} %copy-done.5), kind=kOutput, calls=%fused_computation.1 | convolution fusion | flops 271580672 | bytes 6883328 | tf_op jit(solution)/shard_map/dot_general | solution.py:11
  130.5 0.1 broadcast_in_dim.63
  130.6 0.2 select_reduce_fusion
  130.8 0.1 mul.51
  130.9 2.5 multiply_convert_fusion
  133.3 0.0 copy-start.11
  133.4 51.9 %all_to_all.21 = bf16[8,64,2048]{2,1,0:T(8,128)(2,1)S(1)} all-to-all(bf16[8,64,2048]{2,1,0:T(8,128)(2,1)S(1)} %bitcast.69), channel_id=1, replica_groups=mesh['dp'=4,'expert'=8] {'expert'}, dimensions={0} | all-to-all | bytes 4194304 | tf_op jit(solution)/shard_map/all_to_all | solution.py:35
  185.3 1.3 copy-done.4
  186.6 3.2 %fusion.1 = bf16[1,704,2048]{2,1,0:T(8,128)(2,1)} fusion(bf16[512,704]{0,1:T(8,128)(2,1)S(1)} %copy-done.11, bf16[512,2048]{1,0:T(8,128)(2,1)S(1)} %bitcast.75), kind=kOutput, calls=%fused_computation.10 | convolution fusion | flops 1477836800 | bytes 5701632 | tf_op jit(solution)/shard_map/dot_general | solution.py:11
  189.9 0.0 reduce-scatter.8.cloned.1.call-update
  189.9 0.2 reduce-scatter.6.cloned.1.call-start
  190.1 5.5 %multiply_convert_fusion.3 = (bf16[512,704]{0,1:T(8,128)(2,1)S(1)}, bf16[512,704]{0,1:T(8,128)(2,1)}) fusion(f32[512,704]{0,1:T(8,128)} %copy-done.14, f32[512,704]{0,1:T(8,128)} %get-tuple-element.11, bf16[512,2048]{1,0:T(8,128)(2,1)} %bitcast.76, bf16[1,704,2048]{2,1,0:T(8,128)(2,1)S(1)} %copy-done), kind=kOutput, calls=%fused_computation.28 | convolution fusion | flops 1481080832 | bytes 9306112 | tf_op jit(solution)/shard_map/dot_general | solution.py:11
  195.7 0.9 copy-done.12
  196.5 3.3 %fusion.3 = bf16[1,2048,704]{1,2,0:T(8,128)(2,1)} fusion(bf16[512,704]{0,1:T(8,128)(2,1)S(1)} %get-tuple-element.8, bf16[512,2048]{1,0:T(8,128)(2,1)S(1)} %bitcast.74), kind=kOutput, calls=%fused_computation.12 | convolution fusion | flops 1477836800 | bytes 5701632 | tf_op jit(solution)/shard_map/dot_general | solution.py:11
  199.8 0.0 reduce-scatter.6.cloned.1.call-update
  199.8 0.0 reduce-scatter.4.cloned.1.call-start
  199.9 5.1 %fusion.2 = bf16[1,2048,704]{1,2,0:T(8,128)(2,1)} fusion(bf16[512,704]{0,1:T(8,128)(2,1)} %get-tuple-element.9, bf16[512,2048]{1,0:T(8,128)(2,1)} %bitcast.73), kind=kOutput, calls=%fused_computation.11 | convolution fusion | flops 1477836800 | bytes 5701632 | tf_op jit(solution)/shard_map/dot_general | solution.py:11
  205.0 0.0 reduce-scatter.4.cloned.1.call-update
  205.0 0.0 copy-start.9
  205.0 0.0 copy-start.13
  205.0 4.4 %fusion.10 = f32[512,2048]{1,0:T(8,128)S(1)} fusion(bf16[512,704]{0,1:T(8,128)(2,1)} %get-tuple-element.9, bf16[1,2048,704]{1,2,0:T(8,128)(2,1)} %param.11), kind=kOutput, calls=%fused_computation.19 | convolution fusion | flops 1476395008 | bytes 7798784 | tf_op jit(solution)/shard_map/dot_general | solution.py:11
  209.5 3.3 %add_convert_fusion = bf16[512,2048]{1,0:T(8,128)(2,1)} fusion(f32[512,2048]{1,0:T(8,128)S(1)} %fusion.10, bf16[512,704]{0,1:T(8,128)(2,1)S(1)} %copy-done.13, bf16[1,2048,704]{1,2,0:T(8,128)(2,1)S(1)} %copy-done.9), kind=kOutput, calls=%fused_computation.2 | convolution fusion | flops 1478492160 | bytes 9895936 | tf_op jit(solution)/shard_map/dot_general | solution.py:11
  212.8 4.3 %all-to-all-start.3 = ((bf16[8,64,2048]{2,1,0:T(8,128)(2,1)}), bf16[8,64,2048]{2,1,0:T(8,128)(2,1)}, u32[]{:S(2)}, u32[]{:S(2)}) async-start(bf16[8,64,2048]{2,1,0:T(8,128)(2,1)} %bitcast.77), calls=%async_computation.3 | async-start | bytes 4194304 | tf_op jit(solution)/shard_map/all_to_all | solution.py:35
  217.2 0.6 select_reduce_fusion.2
  217.8 3.0 fusion.14
  220.8 43.5 %all-to-all-done.3 = bf16[8,64,2048]{2,1,0:T(8,128)(2,1)} async-done(((bf16[8,64,2048]{2,1,0:T(8,128)(2,1)}), bf16[8,64,2048]{2,1,0:T(8,128)(2,1)}, u32[]{:S(2)}, u32[]{:S(2)}) %all-to-all-start.3) | async-done | bytes 2097184 | tf_op jit(solution)/shard_map/all_to_all | solution.py:35
  264.3 2.9 fusion.15
  267.2 2.4 convert_element_type.103
  269.6 2.4 convert_element_type.100
  272.0 31.4 %reduce-scatter.4.cloned.1.call-done = bf16[1,512,704]{1,2,0:T(8,128)(2,1)} async-done(((bf16[1,2048,704]{1,2,0:T(8,128)(2,1)}), bf16[1,512,704]{1,2,0:T(8,128)(2,1)}) %reduce-scatter.4.cloned.1.call-update) | async-done | bytes 720912 | tf_op jit(solution)/shard_map/reduce_scatter | solution.py:56
  303.4 2.4 convert_element_type.97
  (24 shorter events, 0.1 us)
Async XLA Ops:
  7.2 64.0 %copy-start = (bf16[1,704,2048]{2,1,0:T(8,128)(2,1)S(1)}, bf16[1,704,2048]{2,1,0:T(8,128)(2,1)}, u32[]{:S(2)}) copy-start(bf16[1,704,2048]{2,1,0:T(8,128)(2,1)} %param.13) | copy-start | bytes 8650756
  10.1 55.6 %copy-start.1 = (bf16[1,2048,704]{1,2,0:T(8,128)(2,1)S(1)}, bf16[1,2048,704]{1,2,0:T(8,128)(2,1)}, u32[]{:S(2)}) copy-start(bf16[1,2048,704]{1,2,0:T(8,128)(2,1)} %param.11) | copy-start | bytes 8650756
  65.7 1.7 copy-start.2
  65.7 2.6 copy-start.8
  68.3 2.9 copy-start.14
  71.2 3.2 %copy-start.10 = (bf16[512,704]{0,1:T(8,128)(2,1)}, bf16[512,704]{0,1:T(8,128)(2,1)S(1)}, u32[]{:S(2)}) copy-start(bf16[512,704]{0,1:T(8,128)(2,1)S(1)} %get-tuple-element.10) | copy-start | bytes 2162692
  74.4 4.6 %copy-start.6 = (s32[128,3]{0,1:T(4,128)S(1)}, s32[128,3]{0,1:T(4,128)}, u32[]{:S(2)}) copy-start(s32[128,3]{0,1:T(4,128)} %param.9) | copy-start | bytes 4612
  74.4 4.6 %copy-start.7 = (f32[128,3]{0,1:T(4,128)S(1)}, f32[128,3]{0,1:T(4,128)}, u32[]{:S(2)}) copy-start(f32[128,3]{0,1:T(4,128)} %param.10) | copy-start | bytes 4612
  74.4 51.9 %copy-start.5 = (bf16[128,2048]{1,0:T(8,128)(2,1)S(1)}, bf16[128,2048]{1,0:T(8,128)(2,1)}, u32[]{:S(2)}) copy-start(bf16[128,2048]{1,0:T(8,128)(2,1)} %param.8) | copy-start | bytes 1572868
  74.4 51.9 %all-to-all-start.1 = ((bf16[8,64,2048]{2,1,0:T(8,128)(2,1)}), bf16[8,64,2048]{2,1,0:T(8,128)(2,1)}, u32[]{:S(2)}, u32[]{:S(2)}) async-start(bf16[8,64,2048]{2,1,0:T(8,128)(2,1)} %bitcast.78), calls=%async_computation.1 | async-start | bytes 4194304 | tf_op jit(solution)/shard_map/all_to_all | solution.py:35
  78.9 188.3 %reduce-scatter.8.cloned.1.call-start = ((), (), s32[]{:S(2)}) async-start(), calls=%async_computation.9 | async-start | bytes 3604480 | tf_op jit(solution)/shard_map/reduce_scatter | solution.py:56
  133.3 53.3 %copy-start.11 = (bf16[512,704]{0,1:T(8,128)(2,1)S(1)}, bf16[512,704]{0,1:T(8,128)(2,1)}, u32[]{:S(2)}) copy-start(bf16[512,704]{0,1:T(8,128)(2,1)} %copy-done.10) | copy-start | bytes 2162692
  185.3 1.3 copy-start.4
  189.9 79.7 %reduce-scatter.6.cloned.1.call-start = ((), (), s32[]{:S(2)}) async-start(), calls=%async_computation.8 | async-start | bytes 3604480 | tf_op jit(solution)/shard_map/reduce_scatter | solution.py:56
  190.1 6.4 %copy-start.3 = (bf16[8,64,2048]{2,1,0:T(8,128)(2,1)S(1)}, bf16[8,64,2048]{2,1,0:T(8,128)(2,1)}, u32[]{:S(2)}) copy-start(bf16[8,64,2048]{2,1,0:T(8,128)(2,1)} %copy-done.2) | copy-start | bytes 6291460
  195.7 0.9 copy-start.12
  199.8 103.6 %reduce-scatter.4.cloned.1.call-start = ((), (), s32[]{:S(2)}) async-start(), calls=%async_computation.7 | async-start | bytes 3604480 | tf_op jit(solution)/shard_map/reduce_scatter | solution.py:56
  205.0 4.5 %copy-start.9 = (bf16[1,2048,704]{1,2,0:T(8,128)(2,1)S(1)}, bf16[1,2048,704]{1,2,0:T(8,128)(2,1)}, u32[]{:S(2)}) copy-start(bf16[1,2048,704]{1,2,0:T(8,128)(2,1)} %param.12) | copy-start | bytes 8650756
  205.0 4.5 %copy-start.13 = (bf16[512,704]{0,1:T(8,128)(2,1)S(1)}, bf16[512,704]{0,1:T(8,128)(2,1)}, u32[]{:S(2)}) copy-start(bf16[512,704]{0,1:T(8,128)(2,1)} %copy-done.12) | copy-start | bytes 2162692
  212.8 51.5 %all-to-all-start.3 = ((bf16[8,64,2048]{2,1,0:T(8,128)(2,1)}), bf16[8,64,2048]{2,1,0:T(8,128)(2,1)}, u32[]{:S(2)}, u32[]{:S(2)}) async-start(bf16[8,64,2048]{2,1,0:T(8,128)(2,1)} %bitcast.77), calls=%async_computation.3 | async-start | bytes 4194304 | tf_op jit(solution)/shard_map/all_to_all | solution.py:35
Sparse Core Ops, SparseCore 0:
  190.0 35.3 reduce-scatter.7
  228.1 36.3 reduce-scatter.5
  267.0 36.2 reduce-scatter.3

commit v3 on v2

--- a/solution.py
+++ b/solution.py
@@ -45,19 +45,34 @@
     sig = jax.nn.sigmoid(gate_pre)
     hidden = (gate_pre * sig * up_pre).astype(BF16)
     result = dot(hidden, w_down, ((1,), (0,))).astype(BF16)
-    back_out = exchange(result)
 
     hidden_grad = dot(grads, w_down, ((1,), (1,)))
     gate_grad = (hidden_grad * up_pre * sig * (1.0 + gate_pre * (1.0 - sig))).astype(BF16)
     up_grad = (hidden_grad * gate_pre * sig).astype(BF16)
 
     def scatter(partial, dim):
-        partial = partial[None].astype(BF16)
-        return lax.psum_scatter(partial, "dp", scatter_dimension=dim, tiled=True).astype(F32)
+        partial = partial.astype(BF16)
+        far = lax.axis_size("dp") // 2
+        shape = partial.shape[:dim] + (far, 2, partial.shape[dim] // far // 2) + partial.shape[dim + 1 :]
+        pairs = [[2 * i, 2 * i + 1] for i in range(far)]
+        half = lax.psum_scatter(
+            partial.reshape(shape), "dp", scatter_dimension=dim + 1, axis_index_groups=pairs
+        )
+        chips = [[2 * i + c for i in range(far)] for c in range(2)]
+        return lax.psum_scatter(
+            half, "dp", scatter_dimension=dim, axis_index_groups=chips
+        ).astype(F32)[None]
 
-    grad_gate = scatter(dot(rows, gate_grad, ((0,), (0,))), 1)
-    grad_up = scatter(dot(rows, up_grad, ((0,), (0,))), 1)
-    grad_down = scatter(dot(hidden, grads, ((0,), (0,))), 2)
+    part_gate = dot(rows, gate_grad, ((0,), (0,))).astype(BF16)
+    part_up = dot(rows, up_grad, ((0,), (0,))).astype(BF16)
+    part_down = dot(hidden, grads, ((0,), (0,))).astype(BF16)
+    result, part_gate, part_up, part_down = lax.optimization_barrier(
+        (result, part_gate, part_up, part_down)
+    )
+    grad_gate = scatter(part_gate, 0)
+    grad_up = scatter(part_up, 0)
+    grad_down = scatter(part_down, 1)
+    back_out = exchange(result)
     route_grad = (
         dot(gate_grad, w_gate, ((1,), (1,))) + dot(up_grad, w_up, ((1,), (1,)))
     ).astype(BF16)

time: 313 us -> 294 us (0.939)
  blocking collectives: 108 us -> 0 us
  waiting for transfers between devices: 122 us -> 169 us
  local copies, waits for them, and re-layouts: 3.37 us -> 26.8 us
  starting transfers between devices: 9.15 us -> 20.1 us
  matrix products: 44.6 us -> 50.8 us
    all_to_all x2 -> x0, blocking collectives: 108 us -> none  [exchange(): lax.all_to_all(values.reshape(experts, capacity, -1), 'expert', split_axi...]
    all_to_all x2 -> x4, waiting for transfers between devices: 90.8 us -> 166 us  [exchange(): lax.all_to_all(values.reshape(experts, capacity, -1), 'expert', split_axi...]
    reduce_scatter x3 -> x6, waiting for transfers between devices: 31.4 us -> 1.52 us  [the longest x3 1.51 us: scatter(): lax.psum_scatter(partial.reshape(shape), 'dp', scatter_dimension=dim + 1,...]
    reshape x0 -> x6, local copies, waits for them, and re-layouts: none -> 26.5 us  [scatter(): partial.reshape(shape)]
    all_to_all x2 -> x4, starting transfers between devices: 8.84 us -> 19.9 us  [exchange(): lax.all_to_all(values.reshape(experts, capacity, -1), 'expert', split_axi...]
    dot_general x14, matrix products: 44.6 us -> 50.8 us  [dot(): lax.dot_general(left, right, (dims, ((), ())), preferred_element_type=F32)]
    convert_element_type x4 -> x3, other arithmetic: 9.69 us -> 7.37 us  [scatter(): return lax.psum_scatter(half, 'dp', scatter_dimension=dim, axis_index_gro...]
  transfers between devices with their start and end apart: 5 -> 10, of which waited for: 3 -> 5; matrix products, arithmetic and copies ran while one was open for 11% -> 17% of each run, Pallas kernels for 0% -> 0%
where the time goes in v3:
time: 294 us; the launch traced here: 293 us
  waiting for transfers between devices  169 us (57%)
  matrix products  50.8 us (17%)
  local copies, waits for them, and re-layouts  26.8 us (9%)
  starting transfers between devices  20.1 us (7%)
  between operations  14.3 us (5%)
  other arithmetic  11.9 us (4%)
    all_to_all x4, waiting for transfers between devices, exchange(): lax.all_to_all(values.reshape(experts, capacity, -1), 'expert', split_axi...  166 us
    dot_general x14, matrix products, dot(): lax.dot_general(left, right, (dims, ((), ())), preferred_element_type=F32)  50.8 us
    reshape x6, local copies, waits for them, and re-layouts, scatter(): partial.reshape(shape)  26.5 us
    all_to_all x4, starting transfers between devices, exchange(): lax.all_to_all(values.reshape(experts, capacity, -1), 'expert', split_axi...  19.9 us
    convert_element_type x3, other arithmetic, scatter(): return lax.psum_scatter(half, 'dp', scatter_dimension=dim, axis_index_gro...  7.37 us
  transfers between devices with their start and end apart: 10, of which 5 were waited for; matrix products, arithmetic and copies ran while one was open for 17% of the time, Pallas kernels for 0%

profile of v3, /device:TPU:0, one launch (start us, length us, event | category | flops | bytes accessed | tf_op | source)
XLA Modules:
  0.0 292.6 jit_solution(14675575615505117437)
XLA Ops:
  7.2 0.8 fusion.23
  8.0 0.1 convolution_convert_fusion.5
  8.2 0.1 eq.46
  8.2 0.1 fusion.18
  8.4 3.1 %convolution_convert_fusion.4 = bf16[512,2048]{1,0:T(8,128)(2,1)} fusion(pred[512,128]{1,0:T(32,128)(4,1)S(1)} %fusion.18, bf16[128,2048]{1,0:T(8,128)(2,1)} %param.7), kind=kOutput, calls=%fused_computation.9 | convolution fusion | flops 269484032 | bytes 2686976 | tf_op jit(solution)/shard_map/dot_general | solution.py:11
  11.4 7.4 %all-to-all-start = ((bf16[8,64,2048]{2,1,0:T(8,128)(2,1)}), bf16[8,64,2048]{2,1,0:T(8,128)(2,1)}, u32[]{:S(2)}, u32[]{:S(2)}) async-start(bf16[8,64,2048]{2,1,0:T(8,128)(2,1)} %bitcast.72), calls=%async_computation | async-start | bytes 4194304 | tf_op jit(solution)/shard_map/all_to_all | solution.py:35
  18.9 0.1 select_reduce_fusion.1
  19.0 0.1 mul.48
  19.1 3.3 %multiply_convert_fusion.1 = (bf16[512,2048]{1,0:T(8,128)(2,1)}, f32[512,2048]{1,0:T(8,128)}) fusion(f32[512]{0:T(512)S(1)} %mul.48, pred[512,128]{1,0:T(32,128)(4,1)S(1)} %fusion.18, bf16[128,2048]{1,0:T(8,128)(2,1)S(1)} %copy-done.5), kind=kOutput, calls=%fused_computation.4 | convolution fusion | flops 270532608 | bytes 6883328 | tf_op jit(solution)/shard_map/dot_general | solution.py:11
  22.4 44.8 %all-to-all-done = bf16[8,64,2048]{2,1,0:T(8,128)(2,1)} async-done(((bf16[8,64,2048]{2,1,0:T(8,128)(2,1)}), bf16[8,64,2048]{2,1,0:T(8,128)(2,1)}, u32[]{:S(2)}, u32[]{:S(2)}) %all-to-all-start) | async-done | bytes 2097184 | tf_op jit(solution)/shard_map/all_to_all | solution.py:35
  67.2 4.3 %all-to-all-start.1 = ((bf16[8,64,2048]{2,1,0:T(8,128)(2,1)}), bf16[8,64,2048]{2,1,0:T(8,128)(2,1)}, u32[]{:S(2)}, u32[]{:S(2)}) async-start(bf16[8,64,2048]{2,1,0:T(8,128)(2,1)} %bitcast.71), calls=%async_computation.1 | async-start | bytes 4194304 | tf_op jit(solution)/shard_map/all_to_all | solution.py:35
  71.6 0.0 reduce-scatter.7.cloned.1.call-start
  71.6 5.4 %fusion.5 = f32[512,704]{0,1:T(8,128)} fusion(bf16[512,2048]{1,0:T(8,128)(2,1)} %bitcast.4, bf16[1,2048,704]{1,2,0:T(8,128)(2,1)} %param.12), kind=kOutput, calls=%fused_computation.14 | convolution fusion | flops 1476395008 | bytes 6422528 | tf_op jit(solution)/shard_map/dot_general | solution.py:11
  77.0 4.4 %fusion.9 = f32[512,704]{0,1:T(8,128)} fusion(bf16[512,2048]{1,0:T(8,128)(2,1)} %bitcast.4, bf16[1,2048,704]{1,2,0:T(8,128)(2,1)S(1)} %copy-done.2), kind=kOutput, calls=%fused_computation.18 | convolution fusion | flops 1476395008 | bytes 6422528 | tf_op jit(solution)/shard_map/dot_general | solution.py:11
  81.4 38.0 %all-to-all-done.1 = bf16[8,64,2048]{2,1,0:T(8,128)(2,1)} async-done(((bf16[8,64,2048]{2,1,0:T(8,128)(2,1)}), bf16[8,64,2048]{2,1,0:T(8,128)(2,1)}, u32[]{:S(2)}, u32[]{:S(2)}) %all-to-all-start.1) | async-done | bytes 2097184 | tf_op jit(solution)/shard_map/all_to_all | solution.py:35
  119.4 4.6 %multiply_convert_fusion.3 = (bf16[512,704]{0,1:T(8,128)(2,1)S(1)}, bf16[512,704]{0,1:T(8,128)(2,1)S(1)}, bf16[512,704]{0,1:T(8,128)(2,1)S(1)}) fusion(f32[512,704]{0,1:T(8,128)} %fusion.9, f32[512,704]{0,1:T(8,128)} %fusion.5, bf16[512,2048]{1,0:T(8,128)(2,1)} %bitcast.10, bf16[1,704,2048]{2,1,0:T(8,128)(2,1)S(1)} %copy-done), kind=kOutput, calls=%fused_computation.25 | convolution fusion | flops 1482162176 | bytes 10027008 | tf_op jit(solution)/shard_map/dot_general | solution.py:11
  124.1 5.5 %convolution_convert_fusion.2 = bf16[704,2048]{1,0:T(8,128)(2,1)} fusion(bf16[512,704]{0,1:T(8,128)(2,1)S(1)} %get-tuple-element.16, bf16[512,2048]{1,0:T(8,128)(2,1)} %bitcast.10), kind=kOutput, calls=%fused_computation.7 | convolution fusion | flops 1477836800 | bytes 5701632 | tf_op jit(solution)/shard_map/dot_general | solution.py:11
  129.5 3.2 %convolution_convert_fusion.3 = bf16[512,2048]{1,0:T(8,128)(2,1)} fusion(bf16[512,704]{0,1:T(8,128)(2,1)S(1)} %get-tuple-element.16, bf16[1,704,2048]{2,1,0:T(8,128)(2,1)S(1)} %copy-done), kind=kOutput, calls=%fused_computation.8 | convolution fusion | flops 1477443584 | bytes 5701632 | tf_op jit(solution)/shard_map/dot_general | solution.py:11
  132.7 4.9 %convolution_convert_fusion = bf16[2048,704]{0,1:T(8,128)(2,1)} fusion(bf16[512,704]{0,1:T(8,128)(2,1)S(1)} %get-tuple-element.14, bf16[512,2048]{1,0:T(8,128)(2,1)} %bitcast.4), kind=kOutput, calls=%fused_computation.5 | convolution fusion | flops 1477836800 | bytes 5701632 | tf_op jit(solution)/shard_map/dot_general | solution.py:11
  137.6 4.9 %convolution_convert_fusion.1 = bf16[2048,704]{0,1:T(8,128)(2,1)} fusion(bf16[512,704]{0,1:T(8,128)(2,1)S(1)} %get-tuple-element.15, bf16[512,2048]{1,0:T(8,128)(2,1)} %bitcast.4), kind=kOutput, calls=%fused_computation.6 | convolution fusion | flops 1477836800 | bytes 5701632 | tf_op jit(solution)/shard_map/dot_general | solution.py:11
  142.5 6.6 %reshape.88 = bf16[2,2,512,704]{2,1,0,3:T(2,128)(2,1)S(1)} reshape(bf16[2048,704]{0,1:T(8,128)(2,1)} %convolution_convert_fusion.1) | data formatting | bytes 5767168 | tf_op jit(solution)/shard_map/reshape | solution.py:59
  149.1 2.1 copy.16
  151.3 0.0 reduce-scatter.15.cloned.1.call-start
  151.3 6.7 %reshape.90 = bf16[704,2,2,512]{3,2,1,0:T(2,128)(2,1)S(1)} reshape(bf16[704,2048]{1,0:T(8,128)(2,1)} %convolution_convert_fusion.2) | data formatting | bytes 5767168 | tf_op jit(solution)/shard_map/reshape | solution.py:59
  158.1 2.2 copy.18
  160.3 0.0 reduce-scatter.11.cloned.1.call-start
  160.3 6.6 %reshape.89 = bf16[2,2,512,704]{2,1,0,3:T(2,128)(2,1)S(1)} reshape(bf16[2048,704]{0,1:T(8,128)(2,1)} %convolution_convert_fusion) | data formatting | bytes 5767168 | tf_op jit(solution)/shard_map/reshape | solution.py:59
  167.0 2.2 copy.17
  169.2 0.0 reduce-scatter.9.cloned.1.call-start
  169.3 0.5 reduce-scatter.9.cloned.1.call-update
  169.8 3.7 %all-to-all-start.2 = ((bf16[8,64,2048]{2,1,0:T(8,128)(2,1)}), bf16[8,64,2048]{2,1,0:T(8,128)(2,1)S(1)}, u32[]{:S(2)}, u32[]{:S(2)}) async-start(bf16[8,64,2048]{2,1,0:T(8,128)(2,1)} %bitcast.73), calls=%async_computation.2 | async-start | bytes 4194304 | tf_op jit(solution)/shard_map/all_to_all | solution.py:35
  173.6 1.5 reduce-scatter.15.cloned.1.call-done
  175.1 3.8 %fusion.7 = f32[512,2048]{1,0:T(8,128)S(1)} fusion(bf16[512,704]{0,1:T(8,128)(2,1)S(1)} %copy-done.4, bf16[1,2048,704]{1,2,0:T(8,128)(2,1)} %param.11), kind=kOutput, calls=%fused_computation.16 | convolution fusion | flops 1476395008 | bytes 7798784 | tf_op jit(solution)/shard_map/dot_general | solution.py:11
  179.0 3.4 %add_convert_fusion = bf16[512,2048]{1,0:T(8,128)(2,1)} fusion(f32[512,2048]{1,0:T(8,128)S(1)} %fusion.7, bf16[512,704]{0,1:T(8,128)(2,1)S(1)} %copy-done.10, bf16[1,2048,704]{1,2,0:T(8,128)(2,1)S(1)} %copy-done.8), kind=kOutput, calls=%fused_computation.2 | convolution fusion | flops 1478492160 | bytes 9895936 | tf_op jit(solution)/shard_map/dot_general | solution.py:11
  182.3 39.5 %all-to-all-done.2 = bf16[8,64,2048]{2,1,0:T(8,128)(2,1)S(1)} async-done(((bf16[8,64,2048]{2,1,0:T(8,128)(2,1)}), bf16[8,64,2048]{2,1,0:T(8,128)(2,1)S(1)}, u32[]{:S(2)}, u32[]{:S(2)}) %all-to-all-start.2) | async-done | bytes 2097184 | tf_op jit(solution)/shard_map/all_to_all | solution.py:35
  221.9 4.4 %all-to-all-start.3 = ((bf16[8,64,2048]{2,1,0:T(8,128)(2,1)}), bf16[8,64,2048]{2,1,0:T(8,128)(2,1)}, u32[]{:S(2)}, u32[]{:S(2)}) async-start(bf16[8,64,2048]{2,1,0:T(8,128)(2,1)} %bitcast.74), calls=%async_computation.3 | async-start | bytes 4194304 | tf_op jit(solution)/shard_map/all_to_all | solution.py:35
  226.3 0.0 reduce-scatter.13.cloned.1.call-start
  226.3 0.5 reduce-scatter.13.cloned.1.call-update
  226.8 2.7 fusion
  229.5 0.1 broadcast_in_dim.63
  229.6 0.1 select_reduce_fusion
  229.7 0.6 select_reduce_fusion.2
  230.3 43.7 %all-to-all-done.3 = bf16[8,64,2048]{2,1,0:T(8,128)(2,1)} async-done(((bf16[8,64,2048]{2,1,0:T(8,128)(2,1)}), bf16[8,64,2048]{2,1,0:T(8,128)(2,1)}, u32[]{:S(2)}, u32[]{:S(2)}) %all-to-all-start.3) | async-done | bytes 2097184 | tf_op jit(solution)/shard_map/all_to_all | solution.py:35
  274.1 2.9 fusion.12
  276.9 1.4 fusion.11
  278.4 2.6 convert_element_type.101
  280.9 2.4 bitcast_convert_fusion
  283.3 2.4 convert_element_type.102
  (34 shorter events, 0.2 us)
Async XLA Ops:
  7.2 112.2 %copy-start = (bf16[1,704,2048]{2,1,0:T(8,128)(2,1)S(1)}, bf16[1,704,2048]{2,1,0:T(8,128)(2,1)}, u32[]{:S(2)}) copy-start(bf16[1,704,2048]{2,1,0:T(8,128)(2,1)} %param.13) | copy-start | bytes 8650756
  11.4 7.4 %copy-start.6 = (s32[128,3]{0,1:T(4,128)S(1)}, s32[128,3]{0,1:T(4,128)}, u32[]{:S(2)}) copy-start(s32[128,3]{0,1:T(4,128)} %param.9) | copy-start | bytes 4612
  11.4 7.4 %copy-start.7 = (f32[128,3]{0,1:T(4,128)S(1)}, f32[128,3]{0,1:T(4,128)}, u32[]{:S(2)}) copy-start(f32[128,3]{0,1:T(4,128)} %param.10) | copy-start | bytes 4612
  11.4 7.7 %copy-start.5 = (bf16[128,2048]{1,0:T(8,128)(2,1)S(1)}, bf16[128,2048]{1,0:T(8,128)(2,1)}, u32[]{:S(2)}) copy-start(bf16[128,2048]{1,0:T(8,128)(2,1)} %param.8) | copy-start | bytes 1572868
  11.4 55.8 %all-to-all-start = ((bf16[8,64,2048]{2,1,0:T(8,128)(2,1)}), bf16[8,64,2048]{2,1,0:T(8,128)(2,1)}, u32[]{:S(2)}, u32[]{:S(2)}) async-start(bf16[8,64,2048]{2,1,0:T(8,128)(2,1)} %bitcast.72), calls=%async_computation | async-start | bytes 4194304 | tf_op jit(solution)/shard_map/all_to_all | solution.py:35
  67.2 52.2 %all-to-all-start.1 = ((bf16[8,64,2048]{2,1,0:T(8,128)(2,1)}), bf16[8,64,2048]{2,1,0:T(8,128)(2,1)}, u32[]{:S(2)}, u32[]{:S(2)}) async-start(bf16[8,64,2048]{2,1,0:T(8,128)(2,1)} %bitcast.71), calls=%async_computation.1 | async-start | bytes 4194304 | tf_op jit(solution)/shard_map/all_to_all | solution.py:35
  71.6 97.7 %reduce-scatter.7.cloned.1.call-start = ((), (), s32[]{:S(2)}) async-start(), calls=%async_computation.10 | async-start | bytes 4325376 | tf_op jit(solution)/shard_map/reduce_scatter | solution.py:58
  71.6 5.4 %copy-start.2 = (bf16[1,2048,704]{1,2,0:T(8,128)(2,1)S(1)}, bf16[1,2048,704]{1,2,0:T(8,128)(2,1)}, u32[]{:S(2)}) copy-start(bf16[1,2048,704]{1,2,0:T(8,128)(2,1)} %param.11) | copy-start | bytes 8650756
  124.0 8.7 %copy-start.9 = (bf16[512,704]{0,1:T(8,128)(2,1)}, bf16[512,704]{0,1:T(8,128)(2,1)S(1)}, u32[]{:S(2)}) copy-start(bf16[512,704]{0,1:T(8,128)(2,1)S(1)} %get-tuple-element.14) | copy-start | bytes 2162692
  124.0 13.6 %copy-start.3 = (bf16[512,704]{0,1:T(8,128)(2,1)}, bf16[512,704]{0,1:T(8,128)(2,1)S(1)}, u32[]{:S(2)}) copy-start(bf16[512,704]{0,1:T(8,128)(2,1)S(1)} %get-tuple-element.15) | copy-start | bytes 2162692
  151.3 23.8 %reduce-scatter.15.cloned.1.call-start = ((), (), s32[]{:S(2)}) async-start(), calls=%async_computation.14 | async-start | bytes 4325376 | tf_op jit(solution)/shard_map/reduce_scatter | solution.py:58
  160.3 66.0 %reduce-scatter.11.cloned.1.call-start = ((), (), s32[]{:S(2)}) async-start(), calls=%async_computation.12 | async-start | bytes 4325376 | tf_op jit(solution)/shard_map/reduce_scatter | solution.py:58
  169.2 109.2 %reduce-scatter.9.cloned.1.call-start = ((), (), s32[]{:S(2)}) async-start(), calls=%async_computation.11 | async-start | bytes 2162688 | tf_op jit(solution)/shard_map/reduce_scatter | solution.py:62
  169.8 5.3 %copy-start.4 = (bf16[512,704]{0,1:T(8,128)(2,1)S(1)}, bf16[512,704]{0,1:T(8,128)(2,1)}, u32[]{:S(2)}) copy-start(bf16[512,704]{0,1:T(8,128)(2,1)} %copy-done.3) | copy-start | bytes 2162692
  169.8 52.1 %all-to-all-start.2 = ((bf16[8,64,2048]{2,1,0:T(8,128)(2,1)}), bf16[8,64,2048]{2,1,0:T(8,128)(2,1)S(1)}, u32[]{:S(2)}, u32[]{:S(2)}) async-start(bf16[8,64,2048]{2,1,0:T(8,128)(2,1)} %bitcast.73), calls=%async_computation.2 | async-start | bytes 4194304 | tf_op jit(solution)/shard_map/all_to_all | solution.py:35
  173.5 107.4 %reduce-scatter.17.cloned.1.call-start = ((), (), s32[]{:S(2)}) async-start(), calls=%async_computation.15 | async-start | bytes 2162688 | tf_op jit(solution)/shard_map/reduce_scatter | solution.py:62
  175.1 3.9 %copy-start.8 = (bf16[1,2048,704]{1,2,0:T(8,128)(2,1)S(1)}, bf16[1,2048,704]{1,2,0:T(8,128)(2,1)}, u32[]{:S(2)}) copy-start(bf16[1,2048,704]{1,2,0:T(8,128)(2,1)} %param.12) | copy-start | bytes 8650756
  175.1 3.9 %copy-start.10 = (bf16[512,704]{0,1:T(8,128)(2,1)S(1)}, bf16[512,704]{0,1:T(8,128)(2,1)}, u32[]{:S(2)}) copy-start(bf16[512,704]{0,1:T(8,128)(2,1)} %copy-done.9) | copy-start | bytes 2162692
  221.9 52.2 %all-to-all-start.3 = ((bf16[8,64,2048]{2,1,0:T(8,128)(2,1)}), bf16[8,64,2048]{2,1,0:T(8,128)(2,1)}, u32[]{:S(2)}, u32[]{:S(2)}) async-start(bf16[8,64,2048]{2,1,0:T(8,128)(2,1)} %bitcast.74), calls=%async_computation.3 | async-start | bytes 4194304 | tf_op jit(solution)/shard_map/all_to_all | solution.py:35
  226.3 57.1 %reduce-scatter.13.cloned.1.call-start = ((), (), s32[]{:S(2)}) async-start(), calls=%async_computation.13 | async-start | bytes 2162688 | tf_op jit(solution)/shard_map/reduce_scatter | solution.py:62
  278.4 7.4 %copy-start.1 = (bf16[1,704,2048]{2,1,0:T(8,128)(2,1)S(1)}, bf16[1,704,2048]{2,1,0:T(8,128)(2,1)}, u32[]{:S(2)}) copy-start(bf16[1,704,2048]{2,1,0:T(8,128)(2,1)} %param.13) | copy-start | bytes 8650756
Sparse Core Ops, SparseCore 0:
  151.4 9.5 reduce-scatter.6
  163.3 11.7 reduce-scatter.14
  177.3 11.7 reduce-scatter.10
  191.2 25.8 reduce-scatter.8
  219.2 24.6 reduce-scatter.16
  246.1 24.6 reduce-scatter.12

commit v4 on v2

--- a/solution.py
+++ b/solution.py
@@ -1,6 +1,10 @@
+import functools
+
 import jax
 import jax.numpy as jnp
 from jax import lax
+from jax.experimental import pallas as pl
+from jax.experimental.pallas import tpu as pltpu
 from jax.sharding import PartitionSpec as P
 
 F32 = jnp.float32
@@ -9,6 +13,193 @@
 
 def dot(left, right, dims):
     return lax.dot_general(left, right, (dims, ((), ())), preferred_element_type=F32)
+
+
+def columns(experts):
+    near = 1 << ((experts.bit_length() - 1) // 2)
+    return experts // near, near
+
+
+def gather_kernel(
+    nz, ny, capacity, tok_ref, ups_ref, plan_ref, out_ref,
+    held, plans, staged, send_sem, recv_sem, psend_sem, precv_sem, ysend_sem, yrecv_sem,
+):
+    me = lax.axis_index("expert")
+    z, y = me // ny, lax.rem(me, ny)
+    steps = 2 * nz
+
+    def step_of(z_to, y_to):
+        return {"expert": z_to * ny + y_to}
+
+    def hop(i, s, k, way):
+        z_to = lax.rem(z + (1 if way == 0 else nz - 1), nz)
+        return pltpu.make_async_remote_copy(
+            held.at[i, s], held.at[i, s], send_sem.at[i, k, way], recv_sem.at[i, s],
+            device_id=step_of(z_to, y), device_id_type=pl.DeviceIdType.MESH,
+        )
+
+    def plan_hop(s, k, way):
+        z_to = lax.rem(z + (1 if way == 0 else nz - 1), nz)
+        return pltpu.make_async_remote_copy(
+            plans.at[s], plans.at[s], psend_sem.at[k, way], precv_sem.at[s],
+            device_id=step_of(z_to, y), device_id_type=pl.DeviceIdType.MESH,
+        )
+
+    def across(i, s, dy):
+        return pltpu.make_async_remote_copy(
+            staged.at[i, s, dy - 1], out_ref.at[i, s * ny + y],
+            ysend_sem.at[i, s, dy - 1], yrecv_sem.at[i, s, dy - 1],
+            device_id=step_of(z, lax.rem(y + dy, ny)), device_id_type=pl.DeviceIdType.MESH,
+        )
+
+    barrier = pltpu.get_barrier_semaphore()
+
+    def greet(z_to, y_to):
+        pl.semaphore_signal(
+            barrier, inc=1, device_id=step_of(z_to, y_to), device_id_type=pl.DeviceIdType.MESH
+        )
+
+    for dy in range(1, ny):
+        greet(z, lax.rem(y + dy, ny))
+
+    greet(lax.rem(z + 1, nz), y)
+    greet(lax.rem(z + nz - 1, nz), y)
+
+    held[0, z] = tok_ref[...]
+    held[1, z] = ups_ref[...]
+    plans[z] = plan_ref[...]
+
+    pl.semaphore_wait(barrier, ny + 1)
+
+    def process(i, s):
+        line = lax.broadcasted_iota(jnp.int32, (capacity, tok_ref.shape[0]), 0).astype(F32)
+        for dy in list(range(1, ny)) + [0]:
+            plan = plans[s, z * ny + lax.rem(y + dy, ny)]
+            hit = line == plan[0:1, :]
+            weight = jnp.where(i == 0, jnp.ones_like(plan[1:2, :]), plan[1:2, :])
+            scale = jnp.sum(jnp.where(hit, weight, 0.0), axis=1, keepdims=True)
+            got = jnp.dot(
+                jnp.where(hit, 1.0, 0.0).astype(BF16), held[i, s], preferred_element_type=F32
+            )
+            value = (got * scale).astype(BF16)
+            if dy == 0:
+                out_ref[i, s * ny + y] = value
+            else:
+                staged[i, s, dy - 1] = value
+                across(i, s, dy).start()
+
+    def body(q, carry):
+        i, k = q // nz, lax.rem(q, nz)
+        low, high = z - k, z + k
+
+        @pl.when(low >= 0)
+        def _():
+            @pl.when(k > 0)
+            def _():
+                @pl.when(i == 0)
+                def _():
+                    plan_hop(low, k, 0).wait_recv()
+
+                hop(i, low, k, 0).wait_recv()
+
+            @pl.when(z < nz - 1)
+            def _():
+                @pl.when(i == 0)
+                def _():
+                    plan_hop(low, k, 0).start()
+
+                hop(i, low, k, 0).start()
+
+        @pl.when(high < nz)
+        def _():
+            @pl.when(k > 0)
+            def _():
+                @pl.when(i == 0)
+                def _():
+                    plan_hop(high, k, 1).wait_recv()
+
+                hop(i, high, k, 1).wait_recv()
+
+            @pl.when(z > 0)
+            def _():
+                @pl.when(i == 0)
+                def _():
+                    plan_hop(high, k, 1).start()
+
+                hop(i, high, k, 1).start()
+
+        @pl.when(low >= 0)
+        def _():
+            process(i, low)
+
+        @pl.when((high < nz) & (k > 0))
+        def _():
+            process(i, high)
+
+        return carry
+
+    lax.fori_loop(0, steps, body, 0)
+
+    def finish(q, carry):
+        i, k = q // nz, lax.rem(q, nz)
+        low, high = z - k, z + k
+
+        @pl.when((low >= 0) & (z < nz - 1))
+        def _():
+            @pl.when(i == 0)
+            def _():
+                plan_hop(low, k, 0).wait_send()
+
+            hop(i, low, k, 0).wait_send()
+
+        @pl.when((high < nz) & (z > 0))
+        def _():
+            @pl.when(i == 0)
+            def _():
+                plan_hop(high, k, 1).wait_send()
+
+            hop(i, high, k, 1).wait_send()
+
+        for dy in range(1, ny):
+            across(i, k, dy).wait_send()
+            across(i, k, dy).wait_recv()
+        return carry
+
+    lax.fori_loop(0, steps, finish, 0)
+
+
+def gather(tokens, upstream, plan, capacity):
+    tok_rows, width = tokens.shape
+    experts = plan.shape[0]
+    nz, ny = columns(experts)
+    peers = max(ny - 1, 1)
+    vmem = pl.BlockSpec(memory_space=pltpu.VMEM)
+    dma = pltpu.SemaphoreType.DMA
+    return pl.pallas_call(
+        functools.partial(gather_kernel, nz, ny, capacity),
+        out_shape=jax.ShapeDtypeStruct((2, experts, capacity, width), BF16),
+        in_specs=[vmem] * 3,
+        out_specs=vmem,
+        scratch_shapes=[
+            pltpu.VMEM((2, nz, tok_rows, width), BF16),
+            pltpu.VMEM((nz, experts, 8, tok_rows), F32),
+            pltpu.VMEM((2, nz, peers, capacity, width), BF16),
+            dma((2, nz, 2)),
+            dma((2, nz)),
+            dma((nz, 2)),
+            dma((nz,)),
+            dma((2, nz, peers)),
+            dma((2, nz, peers)),
+        ],
+        compiler_params=pltpu.CompilerParams(
+            collective_id=0, has_side_effects=True, vmem_limit_bytes=48 << 20
+        ),
+        cost_estimate=pl.CostEstimate(
+            flops=2 * 2 * experts * capacity * tok_rows * width,
+            bytes_accessed=2 * experts * capacity * width * 2 * 4,
+            transcendentals=0,
+        ),
+    )(tokens, upstream, plan)
 
 
 def shards(tokens, upstream, expert_ids, gate_probs, w_gate, w_up, w_down):
@@ -36,28 +227,36 @@
             values.reshape(experts, capacity, -1), "expert", split_axis=0, concat_axis=0, tiled=True
         ).reshape(experts * capacity, -1)
 
-    rows = exchange(dot(select, tokens, ((1,), (0,))).astype(BF16))
-    out_grad = dot(select, upstream, ((1,), (0,))) * send_probs.reshape(-1, 1)
-    grads = exchange(out_grad.astype(BF16))
+    code = jnp.where(routed, slot, -1).astype(F32)
+    plan = jnp.stack([code, dense] + [jnp.zeros_like(dense)] * 6, axis=1)
+    sent = gather(tokens, upstream, plan, capacity)
+    rows = sent[0].reshape(experts * capacity, width)
+    grads = sent[1].reshape(experts * capacity, width)
 
     gate_pre = dot(rows, w_gate, ((1,), (0,)))
     up_pre = dot(rows, w_up, ((1,), (0,)))
     sig = jax.nn.sigmoid(gate_pre)
     hidden = (gate_pre * sig * up_pre).astype(BF16)
     result = dot(hidden, w_down, ((1,), (0,))).astype(BF16)
-    back_out = exchange(result)
 
     hidden_grad = dot(grads, w_down, ((1,), (1,)))
     gate_grad = (hidden_grad * up_pre * sig * (1.0 + gate_pre * (1.0 - sig))).astype(BF16)
     up_grad = (hidden_grad * gate_pre * sig).astype(BF16)
 
     def scatter(partial, dim):
-        partial = partial[None].astype(BF16)
+        partial = partial[None]
         return lax.psum_scatter(partial, "dp", scatter_dimension=dim, tiled=True).astype(F32)
 
-    grad_gate = scatter(dot(rows, gate_grad, ((0,), (0,))), 1)
-    grad_up = scatter(dot(rows, up_grad, ((0,), (0,))), 1)
-    grad_down = scatter(dot(hidden, grads, ((0,), (0,))), 2)
+    part_gate = dot(rows, gate_grad, ((0,), (0,))).astype(BF16)
+    part_up = dot(rows, up_grad, ((0,), (0,))).astype(BF16)
+    part_down = dot(hidden, grads, ((0,), (0,))).astype(BF16)
+    result, part_gate, part_up, part_down = lax.optimization_barrier(
+        (result, part_gate, part_up, part_down)
+    )
+    grad_gate = scatter(part_gate, 1)
+    grad_up = scatter(part_up, 1)
+    grad_down = scatter(part_down, 2)
+    back_out = exchange(result)
     route_grad = (
         dot(gate_grad, w_gate, ((1,), (1,))) + dot(up_grad, w_up, ((1,), (1,)))
     ).astype(BF16)

time: 313 us -> 238 us (0.76)
  blocking collectives: 108 us -> 0 us
  Pallas kernels: 0 us -> 83.7 us
  waiting for transfers between devices: 122 us -> 81.1 us
  matrix products: 44.6 us -> 35.5 us
    all_to_all x2 -> x0, blocking collectives: 108 us -> none  [exchange(): lax.all_to_all(values.reshape(experts, capacity, -1), 'expert', split_axi...]
    pallas_call x0 -> x1, Pallas kernels: none -> 83.7 us  [gather(): pl.pallas_call(functools.partial(gather_kernel, nz, ny, capacity), out_sh...]
    reduce_scatter x3, waiting for transfers between devices: 31.4 us -> 0.44 us  [scatter(): lax.psum_scatter(partial, 'dp', scatter_dimension=dim, tiled=True)]
    all_to_all x2, waiting for transfers between devices: 90.8 us -> 79.5 us  [exchange(): lax.all_to_all(values.reshape(experts, capacity, -1), 'expert', split_axi...]
    dot_general x14 -> x13, matrix products: 44.6 us -> 35.5 us  [dot(): lax.dot_general(left, right, (dims, ((), ())), preferred_element_type=F32)]
  transfers between devices with their start and end apart: 5 -> 5, of which waited for: 3 -> 3; matrix products, arithmetic and copies ran while one was open for 11% -> 9% of each run, Pallas kernels for 0% -> 0%
where the time goes in v4:
time: 238 us; the launch traced here: 237 us
  Pallas kernels  83.7 us (35%)
  waiting for transfers between devices  81.1 us (34%)
  matrix products  35.5 us (15%)
  between operations  13.9 us (6%)
  other arithmetic  9.81 us (4%)
  starting transfers between devices  9.15 us (4%)
  local copies, waits for them, and re-layouts  4.32 us (2%)
    pallas_call x1, Pallas kernels, gather(): pl.pallas_call(functools.partial(gather_kernel, nz, ny, capacity), out_sh...  83.7 us
    all_to_all x2, waiting for transfers between devices, exchange(): lax.all_to_all(values.reshape(experts, capacity, -1), 'expert', split_axi...  79.5 us
    dot_general x13, matrix products, dot(): lax.dot_general(left, right, (dims, ((), ())), preferred_element_type=F32)  35.5 us
    all_to_all x2, starting transfers between devices, exchange(): lax.all_to_all(values.reshape(experts, capacity, -1), 'expert', split_axi...  8.85 us
    convert_element_type x3, other arithmetic, scatter(): lax.psum_scatter(partial, 'dp', scatter_dimension=dim, tiled=True)  7.22 us
  transfers between devices with their start and end apart: 5, of which 3 were waited for; matrix products, arithmetic and copies ran while one was open for 9% of the time, Pallas kernels for 0%

profile of v4, /device:TPU:0, one launch (start us, length us, event | category | flops | bytes accessed | tf_op | source)
XLA Modules:
  0.0 237.5 jit_solution(3542472380082333749)
XLA Ops:
  7.2 0.0 copy-start
  7.2 0.0 reduce-scatter.4.cloned.1.call-start
  7.2 0.8 fusion.23
  8.1 0.1 select_convert_fusion
  8.2 0.7 select_reduce_fusion.3
  8.9 0.1 pad.2.clone
  9.0 0.1 pad.3.clone
  9.1 0.1 maximum_maximum_fusion.plan_ref
  9.2 1.0 copy-done.1
  10.2 1.0 copy-done.2
  11.2 83.7 %shard_map.118 = bf16[2,8,64,2048]{3,2,1,0:T(8,128)(2,1)S(1)} custom-call(bf16[128,2048]{1,0:T(8,128)(2,1)S(1)} %copy-done.1, bf16[128,2048]{1,0:T(8,128)(2,1)S(1)} %copy-done.2, f32[8,8,128]{2,1,0:T(8,128)S(1)} %maximum_maximum_fusion.plan_ref), custom_call_target="tpu_custom_call" | custom-call | flops 536870912 | bytes 16777216 | tf_op jit(solution)/shard_map/pallas_call | solution.py:178
  94.9 0.0 copy-start.7
  94.9 0.5 fusion.24
  95.4 1.3 copy-done.7
  96.7 1.8 fusion.5
  98.5 0.1 copy-done.4
  98.5 1.7 fusion.9
  100.2 2.3 multiply_convert_fusion.2
  102.6 0.0 copy-start.9
  102.6 3.2 %convolution_convert_fusion.2 = bf16[704,2048]{1,0:T(8,128)(2,1)} fusion(bf16[512,704]{0,1:T(8,128)(2,1)S(1)} %get-tuple-element.20, bf16[512,2048]{1,0:T(8,128)(2,1)S(1)} %bitcast.68), kind=kOutput, calls=%fused_computation.6 | convolution fusion | flops 1477836800 | bytes 5701632 | tf_op jit(solution)/shard_map/dot_general | solution.py:15
  105.8 3.2 %convolution_convert_fusion.3 = bf16[512,2048]{1,0:T(8,128)(2,1)} fusion(bf16[512,704]{0,1:T(8,128)(2,1)S(1)} %get-tuple-element.20, bf16[1,704,2048]{2,1,0:T(8,128)(2,1)S(1)} %copy-done), kind=kOutput, calls=%fused_computation.7 | convolution fusion | flops 1477443584 | bytes 5701632 | tf_op jit(solution)/shard_map/dot_general | solution.py:15
  109.1 3.3 %convolution_convert_fusion = bf16[2048,704]{0,1:T(8,128)(2,1)} fusion(bf16[512,704]{0,1:T(8,128)(2,1)S(1)} %get-tuple-element.18, bf16[512,2048]{1,0:T(8,128)(2,1)S(1)} %bitcast.65), kind=kOutput, calls=%fused_computation.4 | convolution fusion | flops 1477836800 | bytes 5701632 | tf_op jit(solution)/shard_map/dot_general | solution.py:15
  112.3 3.2 %convolution_convert_fusion.1 = bf16[2048,704]{0,1:T(8,128)(2,1)} fusion(bf16[512,704]{0,1:T(8,128)(2,1)S(1)} %get-tuple-element.19, bf16[512,2048]{1,0:T(8,128)(2,1)S(1)} %bitcast.66), kind=kOutput, calls=%fused_computation.5 | convolution fusion | flops 1477836800 | bytes 5701632 | tf_op jit(solution)/shard_map/dot_general | solution.py:15
  115.6 0.0 reduce-scatter.4.cloned.1.call-update
  115.6 0.0 reduce-scatter.6.cloned.1.call-start
  115.7 0.7 reduce-scatter.6.cloned.1.call-update
  116.4 4.4 %all-to-all-start = ((bf16[8,64,2048]{2,1,0:T(8,128)(2,1)}), bf16[8,64,2048]{2,1,0:T(8,128)(2,1)}, u32[]{:S(2)}, u32[]{:S(2)}) async-start(bf16[8,64,2048]{2,1,0:T(8,128)(2,1)} %bitcast.61), calls=%async_computation | async-start | bytes 4194304 | tf_op jit(solution)/shard_map/all_to_all | solution.py:226
  120.8 0.2 reduce-scatter.8.cloned.1.call-start
  121.0 0.5 reduce-scatter.8.cloned.1.call-update
  121.5 0.0 copy-start.10
  121.5 4.5 %fusion.7 = f32[512,2048]{1,0:T(8,128)S(1)} fusion(bf16[512,704]{0,1:T(8,128)(2,1)} %copy-done.5, bf16[1,2048,704]{1,2,0:T(8,128)(2,1)} %param.11), kind=kOutput, calls=%fused_computation.14 | convolution fusion | flops 1476395008 | bytes 7798784 | tf_op jit(solution)/shard_map/dot_general | solution.py:15
  126.0 3.3 %add_convert_fusion = bf16[512,2048]{1,0:T(8,128)(2,1)} fusion(f32[512,2048]{1,0:T(8,128)S(1)} %fusion.7, bf16[512,704]{0,1:T(8,128)(2,1)S(1)} %copy-done.10, bf16[1,2048,704]{1,2,0:T(8,128)(2,1)S(1)} %copy-done.8), kind=kOutput, calls=%fused_computation.2 | convolution fusion | flops 1478492160 | bytes 9895936 | tf_op jit(solution)/shard_map/dot_general | solution.py:15
  129.4 35.9 %all-to-all-done = bf16[8,64,2048]{2,1,0:T(8,128)(2,1)} async-done(((bf16[8,64,2048]{2,1,0:T(8,128)(2,1)}), bf16[8,64,2048]{2,1,0:T(8,128)(2,1)}, u32[]{:S(2)}, u32[]{:S(2)}) %all-to-all-start) | async-done | bytes 2097184 | tf_op jit(solution)/shard_map/all_to_all | solution.py:226
  165.3 4.5 %all-to-all-start.1 = ((bf16[8,64,2048]{2,1,0:T(8,128)(2,1)}), bf16[8,64,2048]{2,1,0:T(8,128)(2,1)}, u32[]{:S(2)}, u32[]{:S(2)}) async-start(bf16[8,64,2048]{2,1,0:T(8,128)(2,1)} %bitcast.62), calls=%async_computation.1 | async-start | bytes 4194304 | tf_op jit(solution)/shard_map/all_to_all | solution.py:226
  169.8 0.0 copy-start.6
  169.8 0.1 eq.46
  169.8 0.1 bitcast_compare_fusion
  170.0 2.8 %fusion = f32[512]{0:T(512)S(1)} fusion(bf16[128,2048]{1,0:T(8,128)(2,1)S(1)} %copy-done.3, bf16[8,64,2048]{2,1,0:T(8,128)(2,1)} %all-to-all-done, pred[512,128]{1,0:T(32,128)(4,1)S(1)} %bitcast.69, pred[512,128]{1,0:T(32,128)(4,1)S(1)} %bitcast_compare_fusion), kind=kOutput, calls=%fused_computation.1 | convolution fusion | flops 271646208 | bytes 2754560 | tf_op jit(solution)/shard_map/dot_general | solution.py:15
  172.8 0.1 broadcast_in_dim.74
  172.9 0.2 select_reduce_fusion
  173.2 0.6 select_reduce_fusion.2
  173.8 43.6 %all-to-all-done.1 = bf16[8,64,2048]{2,1,0:T(8,128)(2,1)} async-done(((bf16[8,64,2048]{2,1,0:T(8,128)(2,1)}), bf16[8,64,2048]{2,1,0:T(8,128)(2,1)}, u32[]{:S(2)}, u32[]{:S(2)}) %all-to-all-start.1) | async-done | bytes 2097184 | tf_op jit(solution)/shard_map/all_to_all | solution.py:226
  217.4 2.9 %fusion.12 = bf16[128,2048]{1,0:T(8,128)(2,1)} fusion(bf16[8,64,2048]{2,1,0:T(8,128)(2,1)} %all-to-all-done.1, s32[8,128]{1,0:T(8,128)S(1)} %get-tuple-element.22, pred[8,128]{1,0:T(8,128)(4,1)S(1)} %fusion.23), kind=kOutput, calls=%fused_computation.21 | convolution fusion | flops 268828672 | bytes 2626560 | tf_op jit(solution)/shard_map/dot_general | solution.py:15
  220.2 3.1 %fusion.11 = bf16[128,2048]{1,0:T(8,128)(2,1)} fusion(f32[8,64]{1,0:T(8,128)S(1)} %get-tuple-element.15, bf16[8,64,2048]{2,1,0:T(8,128)(2,1)} %all-to-all-done, s32[8,128]{1,0:T(8,128)S(1)} %get-tuple-element.22, pred[8,128]{1,0:T(8,128)(4,1)S(1)} %fusion.23), kind=kOutput, calls=%fused_computation.20 | convolution fusion | flops 271974400 | bytes 2628608 | tf_op jit(solution)/shard_map/dot_general | solution.py:15
  223.3 2.4 %convert_element_type.85 = f32[1,512,704]{1,2,0:T(8,128)} convert(bf16[1,512,704]{1,2,0:T(8,128)(2,1)} %reduce-scatter.4.cloned.1.call-done) | non-fusion elementwise | flops 360448 | bytes 2162688 | tf_op jit(solution)/shard_map/convert_element_type | solution.py:248
  225.7 2.4 %convert_element_type.86 = f32[1,512,704]{1,2,0:T(8,128)} convert(bf16[1,512,704]{1,2,0:T(8,128)(2,1)} %reduce-scatter.6.cloned.1.call-done) | non-fusion elementwise | flops 360448 | bytes 2162688 | tf_op jit(solution)/shard_map/convert_element_type | solution.py:248
  228.1 0.4 reduce-scatter.8.cloned.1.call-done
  228.6 2.4 %convert_element_type.87 = f32[1,704,512]{2,1,0:T(8,128)} convert(bf16[1,704,512]{2,1,0:T(8,128)(2,1)} %reduce-scatter.8.cloned.1.call-done) | non-fusion elementwise | flops 360448 | bytes 2162688 | tf_op jit(solution)/shard_map/convert_element_type | solution.py:248
  (19 shorter events, 0.1 us)
Async XLA Ops:
  7.2 93.1 %copy-start = (bf16[1,704,2048]{2,1,0:T(8,128)(2,1)S(1)}, bf16[1,704,2048]{2,1,0:T(8,128)(2,1)}, u32[]{:S(2)}) copy-start(bf16[1,704,2048]{2,1,0:T(8,128)(2,1)} %param.13) | copy-start | bytes 8650756
  7.2 216.1 %reduce-scatter.4.cloned.1.call-start = ((), (), s32[]{:S(2)}) async-start(), calls=%async_computation.5 | async-start | bytes 3604480 | tf_op jit(solution)/shard_map/reduce_scatter | solution.py:248
  9.2 1.0 copy-start.1
  10.2 1.0 copy-start.2
  94.9 1.8 copy-start.7
  96.7 1.8 copy-start.4
  102.6 6.5 %copy-start.9 = (bf16[512,704]{0,1:T(8,128)(2,1)}, bf16[512,704]{0,1:T(8,128)(2,1)S(1)}, u32[]{:S(2)}) copy-start(bf16[512,704]{0,1:T(8,128)(2,1)S(1)} %get-tuple-element.18) | copy-start | bytes 2162692
  102.6 9.8 %copy-start.5 = (bf16[512,704]{0,1:T(8,128)(2,1)}, bf16[512,704]{0,1:T(8,128)(2,1)S(1)}, u32[]{:S(2)}) copy-start(bf16[512,704]{0,1:T(8,128)(2,1)S(1)} %get-tuple-element.19) | copy-start | bytes 2162692
  115.6 110.1 %reduce-scatter.6.cloned.1.call-start = ((), (), s32[]{:S(2)}) async-start(), calls=%async_computation.6 | async-start | bytes 3604480 | tf_op jit(solution)/shard_map/reduce_scatter | solution.py:248
  116.4 48.9 %all-to-all-start = ((bf16[8,64,2048]{2,1,0:T(8,128)(2,1)}), bf16[8,64,2048]{2,1,0:T(8,128)(2,1)}, u32[]{:S(2)}, u32[]{:S(2)}) async-start(bf16[8,64,2048]{2,1,0:T(8,128)(2,1)} %bitcast.61), calls=%async_computation | async-start | bytes 4194304 | tf_op jit(solution)/shard_map/all_to_all | solution.py:226
  120.8 107.8 %reduce-scatter.8.cloned.1.call-start = ((), (), s32[]{:S(2)}) async-start(), calls=%async_computation.7 | async-start | bytes 3604480 | tf_op jit(solution)/shard_map/reduce_scatter | solution.py:248
  121.5 4.5 %copy-start.8 = (bf16[1,2048,704]{1,2,0:T(8,128)(2,1)S(1)}, bf16[1,2048,704]{1,2,0:T(8,128)(2,1)}, u32[]{:S(2)}) copy-start(bf16[1,2048,704]{1,2,0:T(8,128)(2,1)} %param.12) | copy-start | bytes 8650756
  121.5 4.5 %copy-start.10 = (bf16[512,704]{0,1:T(8,128)(2,1)S(1)}, bf16[512,704]{0,1:T(8,128)(2,1)}, u32[]{:S(2)}) copy-start(bf16[512,704]{0,1:T(8,128)(2,1)} %copy-done.9) | copy-start | bytes 2162692
  165.3 4.8 %copy-start.3 = (bf16[128,2048]{1,0:T(8,128)(2,1)S(1)}, bf16[128,2048]{1,0:T(8,128)(2,1)}, u32[]{:S(2)}) copy-start(bf16[128,2048]{1,0:T(8,128)(2,1)} %ups_ref.1) | copy-start | bytes 1572868
  165.3 52.1 %all-to-all-start.1 = ((bf16[8,64,2048]{2,1,0:T(8,128)(2,1)}), bf16[8,64,2048]{2,1,0:T(8,128)(2,1)}, u32[]{:S(2)}, u32[]{:S(2)}) async-start(bf16[8,64,2048]{2,1,0:T(8,128)(2,1)} %bitcast.62), calls=%async_computation.1 | async-start | bytes 4194304 | tf_op jit(solution)/shard_map/all_to_all | solution.py:226
  169.8 3.4 %copy-start.6 = (s32[128,3]{0,1:T(4,128)S(1)}, s32[128,3]{0,1:T(4,128)}, u32[]{:S(2)}) copy-start(s32[128,3]{0,1:T(4,128)} %param.9) | copy-start | bytes 4612
Sparse Core Ops, SparseCore 0:
  115.7 34.8 reduce-scatter.3
  153.3 36.3 reduce-scatter.5
  192.2 36.3 reduce-scatter.7

commit v5 on v4

--- a/solution.py
+++ b/solution.py
@@ -89,7 +89,7 @@
                 across(i, s, dy).start()
 
     def body(q, carry):
-        i, k = q // nz, lax.rem(q, nz)
+        i, k = lax.rem(q, 2), q // 2
         low, high = z - k, z + k
 
         @pl.when(low >= 0)
@@ -250,9 +250,7 @@
     part_gate = dot(rows, gate_grad, ((0,), (0,))).astype(BF16)
     part_up = dot(rows, up_grad, ((0,), (0,))).astype(BF16)
     part_down = dot(hidden, grads, ((0,), (0,))).astype(BF16)
-    result, part_gate, part_up, part_down = lax.optimization_barrier(
-        (result, part_gate, part_up, part_down)
-    )
+    result, _ = lax.optimization_barrier((result, part_gate))
     grad_gate = scatter(part_gate, 1)
     grad_up = scatter(part_up, 1)
     grad_down = scatter(part_down, 2)

time: 238 us -> 241 us (1.013)
  matrix products: 35.5 us -> 40.3 us
  waiting for transfers between devices: 81.1 us -> 78.5 us
    dot_general x13, matrix products: 35.5 us -> 40.3 us  [dot(): lax.dot_general(left, right, (dims, ((), ())), preferred_element_type=F32)]
  transfers between devices with their start and end apart: 5 -> 5, of which waited for: 3 -> 2; matrix products, arithmetic and copies ran while one was open for 9% -> 15% of each run, Pallas kernels for 0% -> 0%
where the time goes in v5:
time: 241 us; the launch traced here: 240 us
  Pallas kernels  82.2 us (34%)
  waiting for transfers between devices  78.5 us (33%)
  matrix products  40.3 us (17%)
  between operations  13.9 us (6%)
  other arithmetic  9.81 us (4%)
  starting transfers between devices  9.15 us (4%)
  local copies, waits for them, and re-layouts  5.91 us (2%)
    pallas_call x1, Pallas kernels, gather(): pl.pallas_call(functools.partial(gather_kernel, nz, ny, capacity), out_sh...  82.2 us
    all_to_all x2, waiting for transfers between devices, exchange(): lax.all_to_all(values.reshape(experts, capacity, -1), 'expert', split_axi...  78.5 us
    dot_general x13, matrix products, dot(): lax.dot_general(left, right, (dims, ((), ())), preferred_element_type=F32)  40.3 us
    all_to_all x2, starting transfers between devices, exchange(): lax.all_to_all(values.reshape(experts, capacity, -1), 'expert', split_axi...  8.85 us
    convert_element_type x3, other arithmetic, scatter(): lax.psum_scatter(partial, 'dp', scatter_dimension=dim, tiled=True)  7.22 us
    unnamed x22, local copies, waits for them, and re-layouts  5.07 us
  transfers between devices with their start and end apart: 5, of which 2 were waited for; matrix products, arithmetic and copies ran while one was open for 15% of the time, Pallas kernels for 0%

profile of v5, /device:TPU:0, one launch (start us, length us, event | category | flops | bytes accessed | tf_op | source)
XLA Modules:
  0.0 239.8 jit_solution(1731668663142124538)
XLA Ops:
  7.2 0.0 copy-start
  7.2 0.0 reduce-scatter.8.cloned.1.call-start
  7.2 0.1 pad.3.clone
  7.3 0.1 pad.2.clone
  7.4 0.8 fusion.25
  8.2 0.7 select_reduce_fusion.3
  8.9 0.1 select_convert_fusion
  9.1 0.1 maximum_maximum_fusion.plan_ref
  9.2 1.0 copy-done.1
  10.2 1.0 copy-done.2
  11.2 82.2 %shard_map.118 = bf16[2,8,64,2048]{3,2,1,0:T(8,128)(2,1)S(1)} custom-call(bf16[128,2048]{1,0:T(8,128)(2,1)S(1)} %copy-done.1, bf16[128,2048]{1,0:T(8,128)(2,1)S(1)} %copy-done.2, f32[8,8,128]{2,1,0:T(8,128)S(1)} %maximum_maximum_fusion.plan_ref), custom_call_target="tpu_custom_call" | custom-call | flops 536870912 | bytes 16777216 | tf_op jit(solution)/shard_map/pallas_call | solution.py:178
  93.4 0.0 copy-start.7
  93.4 0.5 fusion.26
  93.9 2.0 copy-done.7
  96.0 1.8 fusion.7
  97.8 0.0 copy-done.4
  97.8 1.7 fusion.11
  99.5 3.4 %multiply_convert_fusion.2 = (bf16[512,704]{0,1:T(8,128)(2,1)}, bf16[512,704]{0,1:T(8,128)(2,1)}, bf16[512,704]{0,1:T(8,128)(2,1)S(1)}) fusion(f32[512,704]{0,1:T(8,128)S(1)} %fusion.11, f32[512,704]{0,1:T(8,128)S(1)} %fusion.7, bf16[512,2048]{1,0:T(8,128)(2,1)S(1)} %bitcast.67, bf16[1,704,2048]{2,1,0:T(8,128)(2,1)S(1)} %copy-done), kind=kOutput, calls=%fused_computation.25 | convolution fusion | flops 1482162176 | bytes 10027008 | tf_op jit(solution)/shard_map/dot_general | solution.py:15
  102.9 0.9 copy-done.9
  103.7 3.3 %fusion.1 = bf16[1,704,2048]{2,1,0:T(8,128)(2,1)} fusion(bf16[512,704]{0,1:T(8,128)(2,1)S(1)} %get-tuple-element.14, bf16[512,2048]{1,0:T(8,128)(2,1)S(1)} %bitcast.68), kind=kOutput, calls=%fused_computation.8 | convolution fusion | flops 1477836800 | bytes 5701632 | tf_op jit(solution)/shard_map/dot_general | solution.py:15
  107.0 0.0 reduce-scatter.8.cloned.1.call-update
  107.1 0.0 reduce-scatter.4.cloned.1.call-start
  107.1 5.1 %convolution_convert_fusion.1 = bf16[2048,704]{0,1:T(8,128)(2,1)} fusion(bf16[512,704]{0,1:T(8,128)(2,1)} %get-tuple-element.13, bf16[512,2048]{1,0:T(8,128)(2,1)} %bitcast.65), kind=kOutput, calls=%fused_computation.5 | convolution fusion | flops 1477836800 | bytes 5701632 | tf_op jit(solution)/shard_map/dot_general | solution.py:15
  112.2 0.0 reduce-scatter.4.cloned.1.call-update
  112.2 4.3 %convolution_convert_fusion.3 = bf16[512,2048]{1,0:T(8,128)(2,1)} fusion(bf16[512,704]{0,1:T(8,128)(2,1)} %copy-done.9, bf16[1,704,2048]{2,1,0:T(8,128)(2,1)S(1)} %copy-done), kind=kOutput, calls=%fused_computation.7 | convolution fusion | flops 1477443584 | bytes 5701632 | tf_op jit(solution)/shard_map/dot_general | solution.py:15
  116.5 4.3 %all-to-all-start = ((bf16[8,64,2048]{2,1,0:T(8,128)(2,1)}), bf16[8,64,2048]{2,1,0:T(8,128)(2,1)}, u32[]{:S(2)}, u32[]{:S(2)}) async-start(bf16[8,64,2048]{2,1,0:T(8,128)(2,1)} %bitcast.62), calls=%async_computation | async-start | bytes 4194304 | tf_op jit(solution)/shard_map/all_to_all | solution.py:226
  120.8 0.2 reduce-scatter.6.cloned.1.call-start
  121.1 5.1 %fusion.2 = bf16[1,2048,704]{1,2,0:T(8,128)(2,1)} fusion(bf16[512,704]{0,1:T(8,128)(2,1)} %get-tuple-element.12, bf16[512,2048]{1,0:T(8,128)(2,1)} %bitcast.66), kind=kOutput, calls=%fused_computation.9 | convolution fusion | flops 1477836800 | bytes 5701632 | tf_op jit(solution)/shard_map/dot_general | solution.py:15
  126.1 0.0 reduce-scatter.6.cloned.1.call-update
  126.2 0.0 copy-start.8
  126.2 0.0 copy-start.10
  126.2 4.0 %fusion.9 = f32[512,2048]{1,0:T(8,128)S(1)} fusion(bf16[512,704]{0,1:T(8,128)(2,1)} %get-tuple-element.13, bf16[1,2048,704]{1,2,0:T(8,128)(2,1)} %param.11), kind=kOutput, calls=%fused_computation.16 | convolution fusion | flops 1476395008 | bytes 7798784 | tf_op jit(solution)/shard_map/dot_general | solution.py:15
  130.3 3.3 %add_convert_fusion = bf16[512,2048]{1,0:T(8,128)(2,1)} fusion(f32[512,2048]{1,0:T(8,128)S(1)} %fusion.9, bf16[512,704]{0,1:T(8,128)(2,1)S(1)} %copy-done.10, bf16[1,2048,704]{1,2,0:T(8,128)(2,1)S(1)} %copy-done.8), kind=kOutput, calls=%fused_computation.2 | convolution fusion | flops 1478492160 | bytes 9895936 | tf_op jit(solution)/shard_map/dot_general | solution.py:15
  133.6 34.3 %all-to-all-done = bf16[8,64,2048]{2,1,0:T(8,128)(2,1)} async-done(((bf16[8,64,2048]{2,1,0:T(8,128)(2,1)}), bf16[8,64,2048]{2,1,0:T(8,128)(2,1)}, u32[]{:S(2)}, u32[]{:S(2)}) %all-to-all-start) | async-done | bytes 2097184 | tf_op jit(solution)/shard_map/all_to_all | solution.py:226
  167.8 4.5 %all-to-all-start.1 = ((bf16[8,64,2048]{2,1,0:T(8,128)(2,1)}), bf16[8,64,2048]{2,1,0:T(8,128)(2,1)}, u32[]{:S(2)}, u32[]{:S(2)}) async-start(bf16[8,64,2048]{2,1,0:T(8,128)(2,1)} %bitcast.61), calls=%async_computation.1 | async-start | bytes 4194304 | tf_op jit(solution)/shard_map/all_to_all | solution.py:226
  172.4 0.0 copy-start.6
  172.4 0.1 eq.46
  172.5 0.1 bitcast_compare_fusion
  172.6 2.4 fusion
  175.0 0.1 broadcast_in_dim.74
  175.1 0.2 select_reduce_fusion
  175.3 0.6 select_reduce_fusion.2
  175.9 44.2 %all-to-all-done.1 = bf16[8,64,2048]{2,1,0:T(8,128)(2,1)} async-done(((bf16[8,64,2048]{2,1,0:T(8,128)(2,1)}), bf16[8,64,2048]{2,1,0:T(8,128)(2,1)}, u32[]{:S(2)}, u32[]{:S(2)}) %all-to-all-start.1) | async-done | bytes 2097184 | tf_op jit(solution)/shard_map/all_to_all | solution.py:226
  220.1 2.9 %fusion.14 = bf16[128,2048]{1,0:T(8,128)(2,1)} fusion(bf16[8,64,2048]{2,1,0:T(8,128)(2,1)} %all-to-all-done.1, s32[8,128]{1,0:T(8,128)S(1)} %get-tuple-element.16, pred[8,128]{1,0:T(8,128)(4,1)S(1)} %fusion.25), kind=kOutput, calls=%fused_computation.23 | convolution fusion | flops 268828672 | bytes 2626560 | tf_op jit(solution)/shard_map/dot_general | solution.py:15
  223.0 3.0 %fusion.13 = bf16[128,2048]{1,0:T(8,128)(2,1)} fusion(f32[8,64]{1,0:T(8,128)S(1)} %get-tuple-element.9, bf16[8,64,2048]{2,1,0:T(8,128)(2,1)} %all-to-all-done, s32[8,128]{1,0:T(8,128)S(1)} %get-tuple-element.16, pred[8,128]{1,0:T(8,128)(4,1)S(1)} %fusion.25), kind=kOutput, calls=%fused_computation.22 | convolution fusion | flops 271974400 | bytes 2628608 | tf_op jit(solution)/shard_map/dot_general | solution.py:15
  226.0 2.4 %convert_element_type.87 = f32[1,704,512]{2,1,0:T(8,128)} convert(bf16[1,704,512]{2,1,0:T(8,128)(2,1)} %reduce-scatter.8.cloned.1.call-done) | non-fusion elementwise | flops 360448 | bytes 2162688 | tf_op jit(solution)/shard_map/convert_element_type | solution.py:248
  228.5 2.4 %convert_element_type.83 = f32[1,512,704]{1,2,0:T(8,128)} convert(bf16[1,512,704]{1,2,0:T(8,128)(2,1)} %reduce-scatter.4.cloned.1.call-done) | non-fusion elementwise | flops 360448 | bytes 2162688 | tf_op jit(solution)/shard_map/convert_element_type | solution.py:248
  230.9 2.4 %convert_element_type.85 = f32[1,512,704]{1,2,0:T(8,128)} convert(bf16[1,512,704]{1,2,0:T(8,128)(2,1)} %reduce-scatter.6.cloned.1.call-done) | non-fusion elementwise | flops 360448 | bytes 2162688 | tf_op jit(solution)/shard_map/convert_element_type | solution.py:248
  (19 shorter events, 0.1 us)
Async XLA Ops:
  7.2 92.3 %copy-start = (bf16[1,704,2048]{2,1,0:T(8,128)(2,1)S(1)}, bf16[1,704,2048]{2,1,0:T(8,128)(2,1)}, u32[]{:S(2)}) copy-start(bf16[1,704,2048]{2,1,0:T(8,128)(2,1)} %param.13) | copy-start | bytes 8650756
  7.2 218.9 %reduce-scatter.8.cloned.1.call-start = ((), (), s32[]{:S(2)}) async-start(), calls=%async_computation.7 | async-start | bytes 3604480 | tf_op jit(solution)/shard_map/reduce_scatter | solution.py:248
  9.2 1.0 copy-start.1
  10.2 1.0 copy-start.2
  93.4 2.6 %copy-start.7 = (bf16[1,2048,704]{1,2,0:T(8,128)(2,1)S(1)}, bf16[1,2048,704]{1,2,0:T(8,128)(2,1)}, u32[]{:S(2)}) copy-start(bf16[1,2048,704]{1,2,0:T(8,128)(2,1)} %param.12) | copy-start | bytes 8650756
  93.9 3.8 %copy-start.5 = (bf16[1,8,64,2048]{3,2,1,0:T(8,128)(2,1)}, bf16[1,8,64,2048]{3,2,1,0:T(8,128)(2,1)S(1)}, u32[]{:S(2)}) copy-start(bf16[1,8,64,2048]{3,2,1,0:T(8,128)(2,1)S(1)} %get-tuple-element.11) | copy-start | bytes 6291460
  96.0 1.8 copy-start.4
  102.9 0.9 copy-start.9
  107.1 121.4 %reduce-scatter.4.cloned.1.call-start = ((), (), s32[]{:S(2)}) async-start(), calls=%async_computation.5 | async-start | bytes 3604480 | tf_op jit(solution)/shard_map/reduce_scatter | solution.py:248
  116.5 51.4 %all-to-all-start = ((bf16[8,64,2048]{2,1,0:T(8,128)(2,1)}), bf16[8,64,2048]{2,1,0:T(8,128)(2,1)}, u32[]{:S(2)}, u32[]{:S(2)}) async-start(bf16[8,64,2048]{2,1,0:T(8,128)(2,1)} %bitcast.62), calls=%async_computation | async-start | bytes 4194304 | tf_op jit(solution)/shard_map/all_to_all | solution.py:226
  120.8 110.0 %reduce-scatter.6.cloned.1.call-start = ((), (), s32[]{:S(2)}) async-start(), calls=%async_computation.6 | async-start | bytes 3604480 | tf_op jit(solution)/shard_map/reduce_scatter | solution.py:248
  126.2 4.1 %copy-start.8 = (bf16[1,2048,704]{1,2,0:T(8,128)(2,1)S(1)}, bf16[1,2048,704]{1,2,0:T(8,128)(2,1)}, u32[]{:S(2)}) copy-start(bf16[1,2048,704]{1,2,0:T(8,128)(2,1)} %param.12) | copy-start | bytes 8650756
  126.2 4.1 %copy-start.10 = (bf16[512,704]{0,1:T(8,128)(2,1)S(1)}, bf16[512,704]{0,1:T(8,128)(2,1)}, u32[]{:S(2)}) copy-start(bf16[512,704]{0,1:T(8,128)(2,1)} %get-tuple-element.12) | copy-start | bytes 2162692
  167.8 4.8 %copy-start.3 = (bf16[128,2048]{1,0:T(8,128)(2,1)S(1)}, bf16[128,2048]{1,0:T(8,128)(2,1)}, u32[]{:S(2)}) copy-start(bf16[128,2048]{1,0:T(8,128)(2,1)} %ups_ref.1) | copy-start | bytes 1572868
  167.8 52.3 %all-to-all-start.1 = ((bf16[8,64,2048]{2,1,0:T(8,128)(2,1)}), bf16[8,64,2048]{2,1,0:T(8,128)(2,1)}, u32[]{:S(2)}, u32[]{:S(2)}) async-start(bf16[8,64,2048]{2,1,0:T(8,128)(2,1)} %bitcast.61), calls=%async_computation.1 | async-start | bytes 4194304 | tf_op jit(solution)/shard_map/all_to_all | solution.py:226
  172.4 3.0 %copy-start.6 = (s32[128,3]{0,1:T(4,128)S(1)}, s32[128,3]{0,1:T(4,128)}, u32[]{:S(2)}) copy-start(s32[128,3]{0,1:T(4,128)} %param.9) | copy-start | bytes 4612
Sparse Core Ops, SparseCore 0:
  107.2 35.5 reduce-scatter.7
  145.4 36.3 reduce-scatter.3
  184.3 36.3 reduce-scatter.5
